TPU v7x, 32 devices: a whole 2x2x4 slice. The times are simulated.
32 devices in a mesh: section: 2 (over x), tile: 16 (over z, y, core).
Axes of the slice: x: 2, y: 2, z: 4, core: 2. Of those that a mesh axis runs over, the one named last changes fastest.
Arguments:
- queries: bfloat16 [2, 8192, 3072], P('section', 'tile')
- key_values: bfloat16 [2, 2, 8192, 3072], P(None, 'section', 'tile')
- neighbours: int32 [64, 8], P('tile'), may hold values from 0 to 63, as said below
- clean_section: int32 [64], P('tile'), may hold values from 0 to 1
Outputs:
- attended: bfloat16 [2, 8192, 3072], P('section', 'tile')
Inputs may be any that keep to these rules, and one draw needn't show every extreme that they name: neighbours[t] names 8 distinct tiles of the span; the first is t itself; all lie on the device that holds t or on the two devices next to it along the closed cycle of tile devices, and every list names a tile of each of those two devices.
All inputs are finite; a program needn't handle non-finite values.
Results may differ from a plain program's by a relative error of at most 0.0047.
Values may be sent and summed in bfloat16 or wider, within the bound.
No kernel may reach another device: no remote copies, remote signals or barrier semaphores. Data moves between devices by JAX's collectives and lax.ppermute only.
A program may use at most 192 MiB of HBM per device.

v0:
```python
import jax
import jax.numpy as jnp
from jax import lax
from jax.sharding import PartitionSpec as P

HEAD = 128
TILE = 128


def extended(block, sides, width):
    for axis, dim in sides:
        count = lax.axis_size(axis)
        forward = [(i, i + 1) for i in range(count - 1)]
        forward.append((count - 1, 0))
        backward = [(target, source) for source, target in forward]
        low = lax.ppermute(
            lax.slice_in_dim(block, block.shape[dim] - width, None, axis=dim), axis, forward
        )
        high = lax.ppermute(lax.slice_in_dim(block, 0, width, axis=dim), axis, backward)
        block = jnp.concatenate([low, block, high], axis=dim)
    return block


def local(queries, key_values, neighbours, clean_section):
    tok_dev = queries.shape[1]
    feat = queries.shape[2]
    tiles_dev = tok_dev // TILE
    cycle_size = lax.axis_size("tile")
    tile_here = lax.axis_index("tile")
    section_here = lax.axis_index("section")
    live_tile = clean_section != section_here
    device_ids = neighbours // tiles_dev
    slot_index = (device_ids - tile_here + 1) % cycle_size * tiles_dev + neighbours % tiles_dev
    listed = neighbours.shape[1]
    head_count = feat // HEAD
    group_size = 4
    columns = group_size * HEAD
    group_count = head_count // group_size
    score_scale = HEAD ** (-0.5)

    def select(window_pair, offset):
        column_part = lax.dynamic_slice_in_dim(window_pair, offset, columns, 2)
        column_part = column_part.reshape(2, 3 * tiles_dev, TILE, group_size, HEAD)
        return jnp.take(column_part, slot_index, axis=1)

    def query_block(query_rows, offset):
        return lax.dynamic_slice_in_dim(query_rows, offset, columns, 1).reshape(
            tiles_dev, TILE, group_size, HEAD
        )

    both_sections = lax.all_gather(key_values, "section", axis=1, tiled=True)
    window = extended(both_sections, (("tile", 2),), tok_dev)
    own_window = lax.dynamic_index_in_dim(window, section_here, 1, keepdims=False)
    cache_window = lax.dynamic_index_in_dim(window, 1 - section_here, 1, keepdims=False)
    slot_ids = jnp.arange(2 * listed)
    live_mask = (slot_ids[None, :] < listed) | live_tile[:, None]

    def attend(group_index):
        offset = group_index * columns
        query_group = query_block(queries[0], offset)
        own_sel = select(own_window, offset)
        cache_sel = select(cache_window, offset)
        keys_sel = jnp.concatenate([own_sel[0], cache_sel[0]], 1)
        values_sel = jnp.concatenate([own_sel[1], cache_sel[1]], 1)
        scores = (
            jnp.einsum(
                "tqhd,tnkhd->thqnk", query_group, keys_sel, preferred_element_type=jnp.float32
            )
            * score_scale
        )
        scores = jnp.where(live_mask[:, None, None, :, None], scores, -1e30)
        maxima = jnp.max(scores, axis=(3, 4), keepdims=True)
        weights = jnp.exp(scores - maxima)
        totals = jnp.sum(weights, axis=(3, 4))
        result = jnp.einsum(
            "thqnk,tnkhd->tqhd",
            weights.astype(jnp.bfloat16),
            values_sel,
            preferred_element_type=jnp.float32,
        )
        result = result / jnp.transpose(totals, (0, 2, 1))[..., None]
        return result.astype(jnp.bfloat16).reshape(tok_dev, columns)

    results = lax.map(attend, jnp.arange(group_count))
    return jnp.transpose(results, (1, 0, 2)).reshape(1, tok_dev, feat)


def solution(mesh):
    placed = (
        P("section", "tile", None),
        P(None, "section", "tile", None),
        P("tile", None),
        P("tile"),
    )
    return jax.shard_map(
        local, mesh=mesh, in_specs=placed, out_specs=P("section", "tile", None), check_vma=False
    )
```

profile of v0, /device:TPU:12, one launch (start us, length us, event | category | flops | bytes accessed | tf_op | source)
XLA Modules:
  0.0 958.8 jit_solution(2303959566666341855)
XLA Ops:
  7.3 154.3 %all-gather.2.cloned.1.call-done = bf16[2,2,512,3072]{3,2,1,0:T(8,128)(2,1)} async-done(((bf16[2,1,512,3072]{3,2,1,0:T(8,128)(2,1)}), bf16[2,2,512,3072]{3,2,1,0:T(8,128)(2,1)}) %all-gather.2.cloned.1.call-update) | async-done | bytes 12582928 | tf_op jit(solution)/shard_map/all_gather | solution.py:51
  164.9 269.7 %collective-permute-done = bf16[2,2,512,3072]{3,2,1,0:T(8,128)(2,1)} collective-permute-done((bf16[2,2,512,3072]{3,2,1,0:T(8,128)(2,1)}, bf16[2,2,512,3072]{3,2,1,0:T(8,128)(2,1)}, u32[]{:S(2)}, u32[]{:S(2)}) %collective-permute-start) | collective-permute-done | bytes 12582944 | tf_op jit(solution)/shard_map/ppermute | solution.py:16
  434.5 10.6 %constant_dynamic-update-slice_fusion.3 = bf16[2,2,1536,3072]{3,2,1,0:T(8,128)(2,1)} fusion(bf16[2,2,512,3072]{3,2,1,0:T(8,128)(2,1)} %collective-permute-done), kind=kLoop, calls=%fused_computation.44 | loop fusion | bytes 25165824
  445.1 5.4 constant_dynamic-update-slice_fusion.2
  450.5 10.8 %constant_dynamic-update-slice_fusion.1 = bf16[2,2,1536,3072]{3,2,1,0:T(8,128)(2,1)} fusion(bf16[2,2,1536,3072]{3,2,1,0:T(8,128)(2,1)} %constant_dynamic-update-slice_fusion.2, bf16[2,2,512,3072]{3,2,1,0:T(8,128)(2,1)} %collective-permute-done.1), kind=kLoop, calls=%fused_computation.42 | loop fusion | bytes 25165824 | tf_op jit(solution)/shard_map/concatenate | solution.py:20
  461.3 25.0 %dynamic-slice_bitcast_fusion = (bf16[2,1536,3072]{2,1,0:T(8,128)(2,1)}, bf16[2,1536,3072]{2,1,0:T(8,128)(2,1)}) fusion(bf16[2,2,1536,3072]{3,2,1,0:T(8,128)(2,1)} %constant_dynamic-update-slice_fusion.1, s32[]{:T(128)S(6)} %select_n.42, s32[]{:T(128)S(6)} %select_n.38), kind=kLoop, calls=%fused_computation.40 | loop fusion | bytes 75497480 | tf_op jit(solution)/shard_map/jit(dynamic_index_in_dim)/squeeze | solution.py:54
  486.3 461.1 %while.11 = (s32[]{:T(128)}, bf16[6,512,512]{1,2,0:T(8,128)(2,1)}, s32[6]{0:T(128)S(1)}, bf16[2,1536,3072]{2,1,0:T(8,128)(2,1)}, s32[4,8]{1,0:T(4,128)S(1)}, /*i...) while((s32[]{:T(128)}, bf16[6,512,512]{1,2,0:T(8,128)(2,1)}, ...), condition=%wide.region_3.5_spmd.clone, body=%wide.region_0.4_spmd.clone.sunk | while | flops 2210919936 | bytes 312522816 | solution.py:84
  487.5 5.1 constant_dynamic-slice_fusion.5
  498.5 5.0 gather_fusion
  503.5 5.5 reshape.83
  511.7 5.0 gather_fusion.1
  516.8 6.8 fusion.46
  523.6 3.8 slice_bitcast_fusion.6
  527.4 3.7 slice_bitcast_fusion.7
  531.1 7.4 pad_maximum_fusion.2
  539.8 4.8 fusion.47
  551.7 9.9 %divide_convert_fusion.2 = bf16[4,128,4,128]{1,3,2,0:T(8,128)(2,1)S(1)} fusion(f32[4,4,128,2048]{2,3,1,0} %copy-done, f32[4,4,128]{2,1,0:T(4,128)S(1)} %get-tuple-element.173, pred[4,16]{1,0:T(4,128)(4,1)S(1)} %broadcast_or_fusion.2, bf16[4,8,128,4,128]{4,2,1,3,0:T(8,128)(2,1)S(1)} %copy-done.1, ...), kind=kOutput, calls=%fused_computation.26.clone.1 | convolution fusion | flops 1095237632 | bytes 25706560 | tf_op jit(solution)/shard_map/while/body/eval_jaxpr/thqnk,tnkhd->tqhd/dot_general | solution.py:75
  564.4 5.1 constant_dynamic-slice_fusion.5
  575.3 5.0 gather_fusion
  580.3 5.5 reshape.83
  588.6 5.0 gather_fusion.1
  593.6 6.8 fusion.46
  600.5 3.8 slice_bitcast_fusion.6
  604.2 3.7 slice_bitcast_fusion.7
  608.0 7.4 pad_maximum_fusion.2
  616.7 4.9 fusion.47
  628.6 9.9 %divide_convert_fusion.2 = bf16[4,128,4,128]{1,3,2,0:T(8,128)(2,1)S(1)} fusion(f32[4,4,128,2048]{2,3,1,0} %copy-done, f32[4,4,128]{2,1,0:T(4,128)S(1)} %get-tuple-element.173, pred[4,16]{1,0:T(4,128)(4,1)S(1)} %broadcast_or_fusion.2, bf16[4,8,128,4,128]{4,2,1,3,0:T(8,128)(2,1)S(1)} %copy-done.1, ...), kind=kOutput, calls=%fused_computation.26.clone.1 | convolution fusion | flops 1095237632 | bytes 25706560 | tf_op jit(solution)/shard_map/while/body/eval_jaxpr/thqnk,tnkhd->tqhd/dot_general | solution.py:75
  641.2 5.1 constant_dynamic-slice_fusion.5
  652.2 5.0 gather_fusion
  657.2 5.5 reshape.83
  665.4 5.0 gather_fusion.1
  670.5 6.8 fusion.46
  677.3 3.8 slice_bitcast_fusion.6
  684.8 7.4 pad_maximum_fusion.2
  693.5 4.8 fusion.47
  705.4 9.9 %divide_convert_fusion.2 = bf16[4,128,4,128]{1,3,2,0:T(8,128)(2,1)S(1)} fusion(f32[4,4,128,2048]{2,3,1,0} %copy-done, f32[4,4,128]{2,1,0:T(4,128)S(1)} %get-tuple-element.173, pred[4,16]{1,0:T(4,128)(4,1)S(1)} %broadcast_or_fusion.2, bf16[4,8,128,4,128]{4,2,1,3,0:T(8,128)(2,1)S(1)} %copy-done.1, ...), kind=kOutput, calls=%fused_computation.26.clone.1 | convolution fusion | flops 1095237632 | bytes 25706560 | tf_op jit(solution)/shard_map/while/body/eval_jaxpr/thqnk,tnkhd->tqhd/dot_general | solution.py:75
  718.1 5.1 constant_dynamic-slice_fusion.5
  729.0 5.0 gather_fusion
  734.0 5.5 reshape.83
  742.3 5.0 gather_fusion.1
  747.3 6.8 fusion.46
  754.2 3.8 slice_bitcast_fusion.6
  761.7 7.4 pad_maximum_fusion.2
  770.4 4.8 fusion.47
  782.3 9.9 %divide_convert_fusion.2 = bf16[4,128,4,128]{1,3,2,0:T(8,128)(2,1)S(1)} fusion(f32[4,4,128,2048]{2,3,1,0} %copy-done, f32[4,4,128]{2,1,0:T(4,128)S(1)} %get-tuple-element.173, pred[4,16]{1,0:T(4,128)(4,1)S(1)} %broadcast_or_fusion.2, bf16[4,8,128,4,128]{4,2,1,3,0:T(8,128)(2,1)S(1)} %copy-done.1, ...), kind=kOutput, calls=%fused_computation.26.clone.1 | convolution fusion | flops 1095237632 | bytes 25706560 | tf_op jit(solution)/shard_map/while/body/eval_jaxpr/thqnk,tnkhd->tqhd/dot_general | solution.py:75
  794.9 5.1 constant_dynamic-slice_fusion.5
  805.8 5.0 gather_fusion
  810.9 5.5 reshape.83
  819.1 5.0 gather_fusion.1
  824.2 6.8 fusion.46
  831.0 3.8 slice_bitcast_fusion.6
  838.5 7.4 pad_maximum_fusion.2
  847.2 4.8 fusion.47
  859.1 9.9 %divide_convert_fusion.2 = bf16[4,128,4,128]{1,3,2,0:T(8,128)(2,1)S(1)} fusion(f32[4,4,128,2048]{2,3,1,0} %copy-done, f32[4,4,128]{2,1,0:T(4,128)S(1)} %get-tuple-element.173, pred[4,16]{1,0:T(4,128)(4,1)S(1)} %broadcast_or_fusion.2, bf16[4,8,128,4,128]{4,2,1,3,0:T(8,128)(2,1)S(1)} %copy-done.1, ...), kind=kOutput, calls=%fused_computation.26.clone.1 | convolution fusion | flops 1095237632 | bytes 25706560 | tf_op jit(solution)/shard_map/while/body/eval_jaxpr/thqnk,tnkhd->tqhd/dot_general | solution.py:75
  871.7 5.1 constant_dynamic-slice_fusion.5
  882.7 5.0 gather_fusion
  887.7 5.5 reshape.83
  895.9 5.0 gather_fusion.1
  901.0 6.8 fusion.46
  907.8 3.8 slice_bitcast_fusion.6
  915.3 7.4 pad_maximum_fusion.2
  924.0 4.9 fusion.47
  936.0 9.9 %divide_convert_fusion.2 = bf16[4,128,4,128]{1,3,2,0:T(8,128)(2,1)S(1)} fusion(f32[4,4,128,2048]{2,3,1,0} %copy-done, f32[4,4,128]{2,1,0:T(4,128)S(1)} %get-tuple-element.173, pred[4,16]{1,0:T(4,128)(4,1)S(1)} %broadcast_or_fusion.2, bf16[4,8,128,4,128]{4,2,1,3,0:T(8,128)(2,1)S(1)} %copy-done.1, ...), kind=kOutput, calls=%fused_computation.26.clone.1 | convolution fusion | flops 1095237632 | bytes 25706560 | tf_op jit(solution)/shard_map/while/body/eval_jaxpr/thqnk,tnkhd->tqhd/dot_general | solution.py:75
  947.3 4.6 copy.33
  (135 shorter events, 132.3 us)
Async XLA Ops:
  6.5 155.0 %all-gather.2.cloned.1.call-start = ((), (), s32[]{:S(2)}) async-start(), calls=%async_computation | async-start | bytes 18874368 | tf_op jit(solution)/shard_map/all_gather | solution.py:51
  161.6 273.0 %collective-permute-start = (bf16[2,2,512,3072]{3,2,1,0:T(8,128)(2,1)}, bf16[2,2,512,3072]{3,2,1,0:T(8,128)(2,1)}, u32[]{:S(2)}, u32[]{:S(2)}) collective-permute-start(bf16[2,2,512,3072]{3,2,1,0:T(8,128)(2,1)} %all-gather.2.cloned.1.call-done), channel_id=1, source_target_pairs={{0,1},{1,2},{2,3},{3,4},{4,5},{5,6},{6,7},{7,8},{8,9},{9,10},{10,1... | collective-permute-start | bytes 37748744 | tf_op jit(solution)/shard_map/ppermute | solution.py:16
  161.6 288.9 %collective-permute-start.1 = (bf16[2,2,512,3072]{3,2,1,0:T(8,128)(2,1)}, bf16[2,2,512,3072]{3,2,1,0:T(8,128)(2,1)}, u32[]{:S(2)}, u32[]{:S(2)}) collective-permute-start(bf16[2,2,512,3072]{3,2,1,0:T(8,128)(2,1)} %all-gather.2.cloned.1.call-done), channel_id=1, source_target_pairs={{1,0},{2,1},{3,2},{4,3},{5,4},{6,5},{7,6},{8,7},{9,8},{10,9},{11,1... | collective-permute-start | bytes 37748744 | tf_op jit(solution)/shard_map/ppermute | solution.py:19
  164.0 281.1 %slice-start = ((s8[12582912]{0:T(1024)(128)(4,1)}), s8[4194304]{0:T(1024)(128)(4,1)S(1)}, s32[]{:S(2)}) async-start(s8[12582912]{0:T(1024)(128)(4,1)} %bitcast.77), calls=%async_computation.1 | async-start | bytes 8388608
  164.8 280.3 %slice-start.1 = ((s8[12582912]{0:T(1024)(128)(4,1)}), s8[4194304]{0:T(1024)(128)(4,1)S(1)}, s32[]{:S(2)}) async-start(s8[12582912]{0:T(1024)(128)(4,1)} %bitcast.77), calls=%async_computation.2 | async-start | bytes 8388608
  164.9 280.3 %slice-start.2 = ((s8[12582912]{0:T(1024)(128)(4,1)}), s8[4194304]{0:T(1024)(128)(4,1)S(1)}, s32[]{:S(2)}) async-start(s8[12582912]{0:T(1024)(128)(4,1)} %bitcast.77), calls=%async_computation.3 | async-start | bytes 8388608
  544.7 7.1 copy-start
  544.7 7.1 copy-start.1
  621.5 7.1 copy-start
  621.5 7.1 copy-start.1
  698.4 7.1 copy-start
  698.4 7.1 copy-start.1
  775.2 7.1 copy-start
  775.2 7.1 copy-start.1
  852.0 7.1 copy-start
  852.0 7.1 copy-start.1
  928.9 7.1 copy-start
  928.9 7.1 copy-start.1
Sparse Core Ops, SparseCore 0:
  8.9 152.6 all-gather.1
where the time goes:
time: 961 us; the launch traced here: 959 us
  waiting for transfers between devices  425 us (44%)
  local copies, waits for them, and re-layouts  317 us (33%)
  other arithmetic  109 us (11%)
  matrix products  88.5 us (9%)
  between operations  13.4 us (1%)
    ppermute x1, waiting for transfers between devices, extended(): lax.ppermute(lax.slice_in_dim(block, block.shape[dim] - width, None, axis...  270 us
    all_gather x1, waiting for transfers between devices, local(): both_sections = lax.all_gather(key_values, 'section', axis=1, tiled=True)  154 us
    reshape x24, local copies, waits for them, and re-layouts, select(): column_part = column_part.reshape(2, 3 * tiles_dev, TILE, group_size, HEAD)  83.6 us
    gather x12, local copies, waits for them, and re-layouts, select(): return jnp.take(column_part, slot_index, axis=1)  60.4 us
    dot_general x6, matrix products, attend(): jnp.einsum('thqnk,tnkhd->tqhd', weights.astype(jnp.bfloat16), values_sel,...  59.5 us
    squeeze x12, local copies, waits for them, and re-layouts, attend(): values_sel = jnp.concatenate([own_sel[1], cache_sel[1]], 1)  45.1 us
    concatenate x6, other arithmetic, attend(): keys_sel = jnp.concatenate([own_sel[0], cache_sel[0]], 1)  44.4 us
    select_n x12, other arithmetic, select(): return jnp.take(column_part, slot_index, axis=1)  40.9 us
  transfers between devices with their start and end apart: 3, of which 2 were waited for; matrix products, arithmetic and copies ran while one was open for 2% of the time, Pallas kernels for 0%

commit v1 on v0

v1 whole, which is shorter than its diff:
```python
import functools
import math

import jax
import jax.numpy as jnp
from jax import lax
from jax.experimental import pallas as pl
from jax.experimental.pallas import tpu as pltpu
from jax.sharding import PartitionSpec as P

HEAD = 128
TILE = 128
LOG2E = math.log2(math.e)
MASKED = -1e30 * LOG2E
SIZES = (3, 4, 4, 4, 4, 3, 2)


def group_sizes(heads):
    if sum(SIZES) == heads:
        return SIZES
    return (heads,) if heads < 4 else (4,) * (heads // 4) + ((heads % 4,) if heads % 4 else ())


def parts_of(x):
    hi = x.astype(jnp.bfloat16).astype(jnp.float32)
    rest = x - hi
    mid = rest.astype(jnp.bfloat16).astype(jnp.float32)
    return hi, mid, rest - mid


def attend_kernel(
    slots_ref, dead_ref, q_ref, qp_ref, own_ref, even_ref, odd_ref,
    out_ref, stat_ref, msg_ref, keys, values, scores, *, tiles, listed, heads, scale,
):
    head = pl.program_id(0)
    columns = pl.ds(pl.multiple_of(head * HEAD, HEAD), HEAD)
    for region, ref in enumerate((own_ref, even_ref, odd_ref)):
        for tile in range(tiles):
            rows = slice(tile * TILE, (tile + 1) * TILE)
            keys[region * tiles + tile] = ref[0, rows, :]
            values[region * tiles + tile] = ref[1, rows, :]
    lane = lax.broadcasted_iota(jnp.int32, (TILE, HEAD), 1)

    @pl.when(head == 0)
    def _():
        stat_ref[...] = jnp.zeros_like(stat_ref)
        msg_ref[:, heads * HEAD :] = jnp.zeros((tiles * TILE, HEAD), msg_ref.dtype)

    def run(tile, query, masked_rows):
        count = query.shape[0]
        base = tile * listed

        def pair(ref, index):
            first = ref[slots_ref[base + 2 * index]]
            second = ref[slots_ref[base + 2 * index + 1]]
            return jnp.concatenate([first, second], 0)

        running = None
        for index in range(listed // 2):
            part = lax.dot_general(
                query, pair(keys, index), (((1,), (1,)), ((), ())),
                preferred_element_type=jnp.float32,
            )
            scores[:count, 2 * index * TILE : 2 * (index + 1) * TILE] = part
            larger = jnp.maximum(part[:, :TILE], part[:, TILE:])
            running = larger if running is None else jnp.maximum(running, larger)
        top = jnp.max(running, axis=1, keepdims=True) * scale
        extra = None
        if masked_rows:
            own_row = lax.broadcasted_iota(jnp.int32, (count, 1), 0) < masked_rows
            top = jnp.where(own_row, jnp.maximum(top, MASKED), top)
            extra = jnp.where(own_row, jnp.exp2(MASKED - top), 0.0)
        total = None
        acc = None
        for index in range(listed // 2):
            part = scores[:count, 2 * index * TILE : 2 * (index + 1) * TILE]
            weight = jnp.exp2(part * scale - top)
            if extra is not None:
                weight = weight + extra
            halves = weight[:, :TILE] + weight[:, TILE:]
            total = halves if total is None else total + halves
            term = lax.dot_general(
                weight.astype(jnp.bfloat16), pair(values, index), (((1,), (0,)), ((), ())),
                preferred_element_type=jnp.float32,
            )
            acc = term if acc is None else acc + term
        total = jnp.sum(total, axis=1, keepdims=True)
        return (acc / total).astype(jnp.bfloat16), top, total

    def one_tile(tile, carry):
        rows = pl.ds(pl.multiple_of(tile * TILE, TILE), TILE)

        @pl.when(dead_ref[tile] == 1)
        def _():
            query = jnp.concatenate([q_ref[rows, :], qp_ref[rows, :]], 0)
            result, top, total = run(tile, query, TILE)
            out_ref[rows, :] = result[:TILE]
            msg_ref[rows, columns] = result[TILE:]
            stats = msg_ref[rows, heads * HEAD :].astype(jnp.float32)
            for k, value in enumerate((*parts_of(top[TILE:]), *parts_of(total[TILE:]))):
                stats = jnp.where(lane == head * 6 + k, value, stats)
            msg_ref[rows, heads * HEAD :] = stats.astype(jnp.bfloat16)

        @pl.when(dead_ref[tile] == 0)
        def _():
            result, top, total = run(tile, q_ref[rows, :], 0)
            out_ref[rows, :] = result
            msg_ref[rows, columns] = jnp.zeros((TILE, HEAD), jnp.bfloat16)
            stats = stat_ref[rows, :]
            stats = jnp.where(lane == head * 2, top, stats)
            stat_ref[rows, :] = jnp.where(lane == head * 2 + 1, total, stats)

        return carry

    lax.fori_loop(0, tiles, one_tile, 0)


def merge_kernel(dead_ref, own_ref, stat_ref, msg_ref, other_ref, *rest, tiles):
    out_ref = rest[-1]
    head = pl.program_id(0)
    lane = lax.broadcasted_iota(jnp.int32, (TILE, HEAD), 1)

    def pick(stats, index):
        return jnp.sum(jnp.where(lane == index, stats, 0.0), axis=1, keepdims=True)

    for tile in range(tiles):
        rows = slice(tile * TILE, (tile + 1) * TILE)

        @pl.when(dead_ref[tile] == 1)
        def _():
            out_ref[rows, :] = own_ref[rows, :]

        @pl.when(dead_ref[tile] == 0)
        def _():
            stats = stat_ref[rows, :]
            others = other_ref[rows, :].astype(jnp.float32)
            top, total = pick(stats, head * 2), pick(stats, head * 2 + 1)
            values = [pick(others, head * 6 + k) for k in range(6)]
            top_o = values[0] + values[1] + values[2]
            total_o = values[3] + values[4] + values[5]
            most = jnp.maximum(top, top_o)
            weight = total * jnp.exp2(top - most)
            weight_o = total_o * jnp.exp2(top_o - most)
            sum_of = weight + weight_o
            result = own_ref[rows, :].astype(jnp.float32) * (weight / sum_of)
            result = result + msg_ref[rows, :].astype(jnp.float32) * (weight_o / sum_of)
            out_ref[rows, :] = result.astype(out_ref.dtype)


def local(queries, key_values, neighbours, clean_section):
    tok_dev, feat = queries.shape[1:]
    tiles = tok_dev // TILE
    listed = neighbours.shape[1]
    heads = feat // HEAD
    cycle = lax.axis_size("tile")
    here = lax.axis_index("tile")
    section = lax.axis_index("section")
    scale = HEAD ** (-0.5) * LOG2E

    query = queries[0]
    own = key_values[:, 0]
    dead = (clean_section == section).astype(jnp.int32)
    device = neighbours // tiles
    region = jnp.where(device == here, 0, jnp.where(device == here + 1 - 2 * (here % 2), 1, 2))
    slots = (region * tiles + neighbours % tiles).reshape(-1)

    even_pairs = [(i, i ^ 1) for i in range(cycle)]
    odd_pairs = [(i, (i + 1) % cycle if i % 2 else (i - 1) % cycle) for i in range(cycle)]
    swap = [(0, 1), (1, 0)]

    even = lax.ppermute(own, "tile", even_pairs)

    sizes = group_sizes(heads)
    starts = [sum(sizes[:g]) for g in range(len(sizes))]
    odd, partner = [], []
    for start, size in zip(starts, sizes):
        low, high = start * HEAD, (start + size) * HEAD
        odd.append(lax.ppermute(own[:, :, low:high], "tile", odd_pairs))
        partner.append(lax.ppermute(query[:, low:high], "section", swap))

    def attend(start, size, odd_part, partner_part):
        units = size * tiles * 2 * TILE * listed * TILE
        return pl.pallas_call(
            functools.partial(
                attend_kernel, tiles=tiles, listed=listed, heads=size, scale=scale
            ),
            grid_spec=pltpu.PrefetchScalarGridSpec(
                num_scalar_prefetch=2,
                grid=(size,),
                in_specs=[
                    pl.BlockSpec((tok_dev, HEAD), lambda h, *_: (0, start + h)),
                    pl.BlockSpec((tok_dev, HEAD), lambda h, *_: (0, h)),
                    pl.BlockSpec((2, tok_dev, HEAD), lambda h, *_: (0, 0, start + h)),
                    pl.BlockSpec((2, tok_dev, HEAD), lambda h, *_: (0, 0, start + h)),
                    pl.BlockSpec((2, tok_dev, HEAD), lambda h, *_: (0, 0, h)),
                ],
                out_specs=[
                    pl.BlockSpec((tok_dev, HEAD), lambda h, *_: (0, h)),
                    pl.BlockSpec((tok_dev, HEAD), lambda h, *_: (0, 0)),
                    pl.BlockSpec((tok_dev, (size + 1) * HEAD), lambda h, *_: (0, 0)),
                ],
                scratch_shapes=[
                    pltpu.VMEM((3 * tiles, TILE, HEAD), jnp.bfloat16),
                    pltpu.VMEM((3 * tiles, TILE, HEAD), jnp.bfloat16),
                    pltpu.VMEM((2 * TILE, listed * TILE), jnp.float32),
                ],
            ),
            out_shape=[
                jax.ShapeDtypeStruct((tok_dev, size * HEAD), jnp.bfloat16),
                jax.ShapeDtypeStruct((tok_dev, HEAD), jnp.float32),
                jax.ShapeDtypeStruct((tok_dev, (size + 1) * HEAD), jnp.bfloat16),
            ],
            cost_estimate=pl.CostEstimate(
                flops=4 * units * HEAD, transcendentals=units,
                bytes_accessed=size * HEAD * tok_dev * 2 * 10,
            ),
            compiler_params=pltpu.CompilerParams(
                dimension_semantics=("arbitrary",), vmem_limit_bytes=24 << 20
            ),
            name="attend",
        )(slots, dead, query, partner_part, own, even, odd_part)

    def merge(start, size, mine, stats, message, target):
        block = pl.BlockSpec((tok_dev, HEAD), lambda h, *_: (0, h))
        last = [] if target is None else [target]
        return pl.pallas_call(
            functools.partial(merge_kernel, tiles=tiles),
            grid_spec=pltpu.PrefetchScalarGridSpec(
                num_scalar_prefetch=1,
                grid=(size,),
                in_specs=[
                    block,
                    pl.BlockSpec((tok_dev, HEAD), lambda h, *_: (0, 0)),
                    block,
                    pl.BlockSpec((tok_dev, HEAD), lambda h, *_: (0, size)),
                ]
                + [pl.BlockSpec(memory_space=pl.ANY)] * len(last),
                out_specs=pl.BlockSpec((tok_dev, HEAD), lambda h, *_: (0, start + h)),
            ),
            out_shape=jax.ShapeDtypeStruct((tok_dev, feat), jnp.bfloat16),
            input_output_aliases={5: 0} if last else {},
            cost_estimate=pl.CostEstimate(
                flops=size * HEAD * tok_dev * 8, transcendentals=0,
                bytes_accessed=size * HEAD * tok_dev * 2 * 3,
            ),
            compiler_params=pltpu.CompilerParams(
                dimension_semantics=("arbitrary",), vmem_limit_bytes=16 << 20
            ),
            name="merge",
        )(dead, mine, stats, message, message, *last)

    target = None
    for g, (start, size) in enumerate(zip(starts, sizes)):
        mine, stats, message = attend(start, size, odd[g], partner[g])
        message = lax.ppermute(message, "section", swap)
        target = merge(start, size, mine, stats, message, target)
    return target[None]


def solution(mesh):
    placed = (
        P("section", "tile", None),
        P(None, "section", "tile", None),
        P("tile", None),
        P("tile"),
    )
    return jax.shard_map(
        local, mesh=mesh, in_specs=placed, out_specs=P("section", "tile", None), check_vma=False
    )
```

time: 961 us -> 231 us (0.24)
  waiting for transfers between devices: 425 us -> 88.7 us
  local copies, waits for them, and re-layouts: 317 us -> 18 us
  other arithmetic: 109 us -> 0.02 us
  Pallas kernels: 0 us -> 101 us
  matrix products: 88.5 us -> 0 us
  starting transfers between devices: 1.75 us -> 26.8 us
  between operations: 13.4 us -> 0.2 us
    ppermute x2 -> x22, waiting for transfers between devices: 270 us -> 88.7 us  [the longest x7 52.6 us: local(): odd.append(lax.ppermute(own[:, :, low:high], 'tile', odd_pairs))]
    all_gather x1 -> x0, waiting for transfers between devices: 154 us -> none  [local(): both_sections = lax.all_gather(key_values, 'section', axis=1, tiled=True)]
    pallas_call x0 -> x14, Pallas kernels: none -> 101 us  [the longest x7 67.6 us: attend(): pl.pallas_call(functools.partial(attend_kernel, tiles=tiles, listed=liste...]
    reshape x31 -> x1, local copies, waits for them, and re-layouts: 89 us -> 0.08 us  [local(): slots = (region * tiles + neighbours % tiles).reshape(-1)]
    squeeze x13 -> x0, local copies, waits for them, and re-layouts: 70.1 us -> none  [the longest x12 45.1 us: attend(): values_sel = jnp.concatenate([own_sel[1], cache_sel[1]], 1)]
    gather x12 -> x0, local copies, waits for them, and re-layouts: 60.4 us -> none  [select(): return jnp.take(column_part, slot_index, axis=1)]
    dot_general x6 -> x0, matrix products: 59.5 us -> none  [attend(): jnp.einsum('thqnk,tnkhd->tqhd', weights.astype(jnp.bfloat16), values_sel,...]
    concatenate x6 -> x0, other arithmetic: 44.4 us -> none  [attend(): keys_sel = jnp.concatenate([own_sel[0], cache_sel[0]], 1)]
  transfers between devices with their start and end apart: 3 -> 22, of which waited for: 2 -> 7; matrix products, arithmetic and copies ran while one was open for 2% -> 5% of each run, Pallas kernels for 0% -> 42%
where the time goes in v1:
time: 231 us; the launch traced here: 235 us
  Pallas kernels  101 us (44%)
  waiting for transfers between devices  88.7 us (38%)
  starting transfers between devices  26.8 us (12%)
  local copies, waits for them, and re-layouts  18 us (8%)
    pallas_call x7, Pallas kernels, attend(): pl.pallas_call(functools.partial(attend_kernel, tiles=tiles, listed=liste...  67.6 us
    ppermute x7, waiting for transfers between devices, local(): odd.append(lax.ppermute(own[:, :, low:high], 'tile', odd_pairs))  52.6 us
    ppermute x7, waiting for transfers between devices, local(): partner.append(lax.ppermute(query[:, low:high], 'section', swap))  36.2 us
    pallas_call x7, Pallas kernels, merge(): pl.pallas_call(functools.partial(merge_kernel, tiles=tiles), grid_spec=pl...  33.5 us
    ppermute x7, starting transfers between devices, local(): message = lax.ppermute(message, 'section', swap)  14.5 us
    ppermute x7, starting transfers between devices, local(): partner.append(lax.ppermute(query[:, low:high], 'section', swap))  12.1 us
    unnamed x30, local copies, waits for them, and re-layouts  7.02 us
    slice x3, local copies, waits for them, and re-layouts, local(): partner.append(lax.ppermute(query[:, low:high], 'section', swap))  5.52 us
  transfers between devices with their start and end apart: 22, of which 7 were waited for; matrix products, arithmetic and copies ran while one was open for 5% of the time, Pallas kernels for 42%

profile of v1, /device:TPU:12, one launch (start us, length us, event | category | flops | bytes accessed | tf_op | source)
XLA Modules:
  0.0 234.8 jit_solution(9776172301358884170)
XLA Ops:
  0.0 0.0 collective-permute-start.1
  0.0 1.1 slice.56
  1.1 1.6 collective-permute-start
  2.7 1.9 fusion.4
  4.6 0.7 collective-permute-start.19
  5.3 2.5 %fusion.5 = (bf16[512,512]{1,0:T(8,128)(2,1)S(1)}, bf16[512,512]{1,0:T(8,128)(2,1)S(1)}, bf16[512,512]{1,0:T(8,128)(2,1)S(1)}, bf16[512,512]{1,0:T(8,128)(2,1)}) fusion(bf16[512,3072]{1,0:T(8,128)(2,1)} %bitcast.16), kind=kLoop, calls=%fused_computation.12 | loop fusion | bytes 4194304 | tf_op jit(solution)/shard_map/slice | solution.py:179
  7.8 1.3 collective-permute-start.16
  9.1 2.2 fusion.3
  11.3 0.0 collective-permute-start.17
  11.3 0.0 collective-permute-done.qp_ref
  11.3 0.7 copy-done.9
  12.0 0.7 collective-permute-start.13
  12.8 6.0 %collective-permute-done.19.qp_ref = bf16[512,384]{1,0:T(8,128)(2,1)S(1)} collective-permute-done((bf16[512,384]{1,0:T(8,128)(2,1)S(1)}, bf16[512,384]{1,0:T(8,128)(2,1)S(1)}, u32[]{:S(2)}, u32[]{:S(2)}) %collective-permute-start.19) | collective-permute-done | bytes 393248 | tf_op jit(solution)/shard_map/ppermute | solution.py:179
  18.7 1.5 collective-permute-start.10
  20.2 9.7 %collective-permute-done.16.qp_ref = bf16[512,512]{1,0:T(8,128)(2,1)S(1)} collective-permute-done((bf16[512,512]{1,0:T(8,128)(2,1)S(1)}, bf16[512,512]{1,0:T(8,128)(2,1)S(1)}, u32[]{:S(2)}, u32[]{:S(2)}) %collective-permute-start.16) | collective-permute-done | bytes 524320 | tf_op jit(solution)/shard_map/ppermute | solution.py:179
  30.0 0.8 copy-done.5
  30.8 0.0 collective-permute-start.14
  30.8 10.4 %collective-permute-done.13.qp_ref = bf16[512,512]{1,0:T(8,128)(2,1)S(1)} collective-permute-done((bf16[512,512]{1,0:T(8,128)(2,1)S(1)}, bf16[512,512]{1,0:T(8,128)(2,1)S(1)}, u32[]{:S(2)}, u32[]{:S(2)}) %collective-permute-start.13) | collective-permute-done | bytes 524320 | tf_op jit(solution)/shard_map/ppermute | solution.py:179
  41.2 0.8 copy-done.7
  42.0 0.0 collective-permute-start.11
  42.0 10.0 %collective-permute-done.10.qp_ref = bf16[512,512]{1,0:T(8,128)(2,1)S(1)} collective-permute-done((bf16[512,512]{1,0:T(8,128)(2,1)S(1)}, bf16[512,512]{1,0:T(8,128)(2,1)S(1)}, u32[]{:S(2)}, u32[]{:S(2)}) %collective-permute-start.10) | collective-permute-done | bytes 524320 | tf_op jit(solution)/shard_map/ppermute | solution.py:179
  52.0 0.8 copy-done.3
  52.9 0.0 collective-permute-start.8
  52.9 1.3 fusion.2
  54.2 1.9 slice.57
  56.0 31.6 %collective-permute-done.17.odd_ref = bf16[2,512,512]{2,1,0:T(8,128)(2,1)} collective-permute-done((bf16[2,512,512]{2,1,0:T(8,128)(2,1)}, bf16[2,512,512]{2,1,0:T(8,128)(2,1)}, u32[]{:S(2)}, u32[]{:S(2)}) %collective-permute-start.17) | collective-permute-done | bytes 1048608 | tf_op jit(solution)/shard_map/ppermute | solution.py:178
  87.6 0.0 collective-permute-start.20
  87.7 0.1 reshape.3.slots_ref
  87.8 16.7 %collective-permute-done.14.odd_ref = bf16[2,512,512]{2,1,0:T(8,128)(2,1)} collective-permute-done((bf16[2,512,512]{2,1,0:T(8,128)(2,1)}, bf16[2,512,512]{2,1,0:T(8,128)(2,1)}, u32[]{:S(2)}, u32[]{:S(2)}) %collective-permute-start.14) | collective-permute-done | bytes 1048608 | tf_op jit(solution)/shard_map/ppermute | solution.py:178
  104.5 0.0 collective-permute-start.5
  104.5 0.0 collective-permute-done.1.even_ref
  104.5 0.7 collective-permute-start.7
  105.2 2.8 %copy-done.1 = bf16[2,1,512,3072]{3,2,1,0:T(8,128)(2,1)S(1)} copy-done((bf16[2,1,512,3072]{3,2,1,0:T(8,128)(2,1)S(1)}, bf16[2,1,512,3072]{3,2,1,0:T(8,128)(2,1)}, u32[]{:S(2)}) %copy-start.1) | copy-done | bytes 6291480
  108.0 1.0 copy-done.6
  109.0 11.0 %attend.12 = (bf16[512,512]{1,0:T(8,128)(2,1)S(1)}, f32[512,128]{1,0:T(8,128)S(1)}, bf16[512,640]{1,0:T(8,128)(2,1)S(1)}) custom-call(s32[32]{0:T(128)S(1)} %reshape.3.slots_ref, s32[4]{0:T(128)S(1)} %compare_convert_fusion.dead_ref, bf16[512,3072]{1,0:T(8,128)(2,1)S(1)} %bitcast.17, bf16[512,512]{1,0:T(8,128)(2,1)S(1)} %copy-done.6, ...), custom_call_target="tpu_custom_call" | custom-call | flops 2147483648 | bytes 5242880 | tf_op jit(solution)/shard_map/attend/pallas_call | solution.py:183
  120.1 11.1 %attend.11 = (bf16[512,512]{1,0:T(8,128)(2,1)S(1)}, f32[512,128]{1,0:T(8,128)S(1)}, bf16[512,640]{1,0:T(8,128)(2,1)S(1)}) custom-call(s32[32]{0:T(128)S(1)} %reshape.3.slots_ref, s32[4]{0:T(128)S(1)} %compare_convert_fusion.dead_ref, bf16[512,3072]{1,0:T(8,128)(2,1)S(1)} %bitcast.18, bf16[512,512]{1,0:T(8,128)(2,1)S(1)} %copy-done.8, ...), custom_call_target="tpu_custom_call" | custom-call | flops 2147483648 | bytes 5242880 | tf_op jit(solution)/shard_map/attend/pallas_call | solution.py:183
  131.2 4.2 %collective-permute-done.20.odd_ref = bf16[2,512,384]{2,1,0:T(8,128)(2,1)} collective-permute-done((bf16[2,512,384]{2,1,0:T(8,128)(2,1)}, bf16[2,512,384]{2,1,0:T(8,128)(2,1)}, u32[]{:S(2)}, u32[]{:S(2)}) %collective-permute-start.20) | collective-permute-done | bytes 786464 | tf_op jit(solution)/shard_map/ppermute | solution.py:178
  135.4 0.2 collective-permute-start.2
  135.6 8.6 %attend.13 = (bf16[512,384]{1,0:T(8,128)(2,1)S(1)}, f32[512,128]{1,0:T(8,128)S(1)}, bf16[512,512]{1,0:T(8,128)(2,1)S(1)}) custom-call(s32[32]{0:T(128)S(1)} %reshape.3.slots_ref, s32[4]{0:T(128)S(1)} %compare_convert_fusion.dead_ref, bf16[512,3072]{1,0:T(8,128)(2,1)S(1)} %bitcast.19, bf16[512,384]{1,0:T(8,128)(2,1)S(1)} %collective-permute-done.19.qp_ref, ...), custom_call_target="tpu_custom_call" | custom-call | flops 1610612736 | bytes 3932160 | tf_op jit(solution)/shard_map/attend/pallas_call | solution.py:183
  144.2 0.0 collective-permute-done.7.qp_ref
  144.2 5.6 %collective-permute-start.4 = (bf16[512,384]{1,0:T(8,128)(2,1)S(1)}, bf16[512,384]{1,0:T(8,128)(2,1)S(1)}, u32[]{:S(2)}, u32[]{:S(2)}) collective-permute-start(bf16[512,384]{1,0:T(8,128)(2,1)S(1)} %copy-done.12), channel_id=1, source_target_pairs={{0,16},{16,0},{1,17},{17,1},{2,18},{18,2},{3,19},{19,3},{4,20},{20... | collective-permute-start | bytes 1179656 | tf_op jit(solution)/shard_map/ppermute | solution.py:179
  149.8 0.0 collective-permute-done.11.odd_ref
  149.8 0.1 collective-permute-start.21
  149.9 0.0 collective-permute-done.8.odd_ref
  149.9 1.9 collective-permute-start.18
  151.9 11.0 %attend.10 = (bf16[512,512]{1,0:T(8,128)(2,1)S(1)}, f32[512,128]{1,0:T(8,128)S(1)}, bf16[512,640]{1,0:T(8,128)(2,1)S(1)}) custom-call(s32[32]{0:T(128)S(1)} %reshape.3.slots_ref, s32[4]{0:T(128)S(1)} %compare_convert_fusion.dead_ref, bf16[512,3072]{1,0:T(8,128)(2,1)S(1)} %bitcast.20, bf16[512,512]{1,0:T(8,128)(2,1)S(1)} %copy-done.4, ...), custom_call_target="tpu_custom_call" | custom-call | flops 2147483648 | bytes 5242880 | tf_op jit(solution)/shard_map/attend/pallas_call | solution.py:183
  162.9 11.0 %attend.9 = (bf16[512,512]{1,0:T(8,128)(2,1)S(1)}, f32[512,128]{1,0:T(8,128)S(1)}, bf16[512,640]{1,0:T(8,128)(2,1)S(1)}) custom-call(s32[32]{0:T(128)S(1)} %reshape.3.slots_ref, s32[4]{0:T(128)S(1)} %compare_convert_fusion.dead_ref, bf16[512,3072]{1,0:T(8,128)(2,1)S(1)} %bitcast.21, bf16[512,512]{1,0:T(8,128)(2,1)S(1)} %collective-permute-done.7.qp_ref, ...), custom_call_target="tpu_custom_call" | custom-call | flops 2147483648 | bytes 5242880 | tf_op jit(solution)/shard_map/attend/pallas_call | solution.py:183
  174.0 6.3 %collective-permute-start.15 = (bf16[512,640]{1,0:T(8,128)(2,1)S(1)}, bf16[512,640]{1,0:T(8,128)(2,1)S(1)}, u32[]{:S(2)}, u32[]{:S(2)}) collective-permute-start(bf16[512,640]{1,0:T(8,128)(2,1)S(1)} %get-tuple-element.40), channel_id=1, source_target_pairs={{0,16},{16,0},{1,17},{17,1},{2,18},{18,2},{3,19},{19,3},{4,20},{20... | collective-permute-start | bytes 1966088 | tf_op jit(solution)/shard_map/ppermute | solution.py:255
  180.3 0.1 collective-permute-start.12
  180.4 0.0 collective-permute-done.5.odd_ref
  180.4 1.9 collective-permute-start.9
  182.4 8.6 %attend.8 = (bf16[512,384]{1,0:T(8,128)(2,1)S(1)}, f32[512,128]{1,0:T(8,128)S(1)}, bf16[512,512]{1,0:T(8,128)(2,1)S(1)}) custom-call(s32[32]{0:T(128)S(1)} %reshape.3.slots_ref, s32[4]{0:T(128)S(1)} %compare_convert_fusion.dead_ref, bf16[512,3072]{1,0:T(8,128)(2,1)S(1)} %bitcast.22, bf16[512,384]{1,0:T(8,128)(2,1)S(1)} %collective-permute-done.4.qp_ref, ...), custom_call_target="tpu_custom_call" | custom-call | flops 1610612736 | bytes 3932160 | tf_op jit(solution)/shard_map/attend/pallas_call | solution.py:183
  191.0 2.5 %collective-permute-start.6 = (bf16[512,512]{1,0:T(8,128)(2,1)S(1)}, bf16[512,512]{1,0:T(8,128)(2,1)S(1)}, u32[]{:S(2)}, u32[]{:S(2)}) collective-permute-start(bf16[512,512]{1,0:T(8,128)(2,1)S(1)} %get-tuple-element.31), channel_id=1, source_target_pairs={{0,16},{16,0},{1,17},{17,1},{2,18},{18,2},{3,19},{19,3},{4,20},{20... | collective-permute-start | bytes 1572872 | tf_op jit(solution)/shard_map/ppermute | solution.py:255
  193.4 6.2 %attend.7 = (bf16[512,256]{1,0:T(8,128)(2,1)S(1)}, f32[512,128]{1,0:T(8,128)S(1)}, bf16[512,384]{1,0:T(8,128)(2,1)S(1)}) custom-call(s32[32]{0:T(128)S(1)} %reshape.3.slots_ref, s32[4]{0:T(128)S(1)} %compare_convert_fusion.dead_ref, bf16[512,3072]{1,0:T(8,128)(2,1)S(1)} %bitcast.23, bf16[512,256]{1,0:T(8,128)(2,1)S(1)} %copy-done.10, ...), custom_call_target="tpu_custom_call" | custom-call | flops 1073741824 | bytes 2621440 | tf_op jit(solution)/shard_map/attend/pallas_call | solution.py:183
  199.6 1.6 collective-permute-start.3
  201.3 4.3 %merge.7.rest_0_ = bf16[512,3072]{1,0:T(8,128)(2,1)} custom-call(s32[4]{0:T(128)S(1)} %compare_convert_fusion.dead_ref, bf16[512,384]{1,0:T(8,128)(2,1)S(1)} %get-tuple-element.44.own_ref, f32[512,128]{1,0:T(8,128)S(1)} %get-tuple-element.45.stat_ref, bf16[512,512]{1,0:T(8,128)(2,1)S(1)} %collective-permute-done.21.msg_ref.other_ref, ...), custom_call_target="tpu_custom_call" | custom-call | flops 1572864 | bytes 1179648 | tf_op jit(solution)/shard_map/merge/pallas_call | solution.py:226
  205.6 5.3 %merge.8.rest_0_ = bf16[512,3072]{1,0:T(8,128)(2,1)} custom-call(s32[4]{0:T(128)S(1)} %compare_convert_fusion.dead_ref, bf16[512,512]{1,0:T(8,128)(2,1)S(1)} %get-tuple-element.41.own_ref, f32[512,128]{1,0:T(8,128)S(1)} %get-tuple-element.42.stat_ref, bf16[512,640]{1,0:T(8,128)(2,1)S(1)} %collective-permute-done.18.msg_ref.other_ref, ...), custom_call_target="tpu_custom_call", output_to_operand_aliasing={{}: (5, {})} | custom-call | flops 2097152 | bytes 1572864 | tf_op jit(solution)/shard_map/merge/pallas_call | solution.py:226
  210.9 5.3 %merge.9.rest_0_ = bf16[512,3072]{1,0:T(8,128)(2,1)} custom-call(s32[4]{0:T(128)S(1)} %compare_convert_fusion.dead_ref, bf16[512,512]{1,0:T(8,128)(2,1)S(1)} %get-tuple-element.38.own_ref, f32[512,128]{1,0:T(8,128)S(1)} %get-tuple-element.39.stat_ref, bf16[512,640]{1,0:T(8,128)(2,1)S(1)} %collective-permute-done.15.msg_ref.other_ref, ...), custom_call_target="tpu_custom_call", output_to_operand_aliasing={{}: (5, {})} | custom-call | flops 2097152 | bytes 1572864 | tf_op jit(solution)/shard_map/merge/pallas_call | solution.py:226
  216.3 0.0 collective-permute-done.12.msg_ref.other_ref
  216.3 5.5 %merge.10.rest_0_ = bf16[512,3072]{1,0:T(8,128)(2,1)} custom-call(s32[4]{0:T(128)S(1)} %compare_convert_fusion.dead_ref, bf16[512,512]{1,0:T(8,128)(2,1)S(1)} %get-tuple-element.35.own_ref, f32[512,128]{1,0:T(8,128)S(1)} %get-tuple-element.36.stat_ref, ...), custom_call_target="tpu_custom_call", output_to_operand_aliasing={{}: (5, {})} | custom-call | flops 2097152 | bytes 1572864 | tf_op jit(solution)/shard_map/merge/pallas_call | solution.py:226
  221.8 0.0 collective-permute-done.9.msg_ref.other_ref
  221.8 5.3 %merge.11.rest_0_ = bf16[512,3072]{1,0:T(8,128)(2,1)} custom-call(s32[4]{0:T(128)S(1)} %compare_convert_fusion.dead_ref, bf16[512,512]{1,0:T(8,128)(2,1)S(1)} %get-tuple-element.32.own_ref, f32[512,128]{1,0:T(8,128)S(1)} %get-tuple-element.33.stat_ref, bf16[512,640]{1,0:T(8,128)(2,1)S(1)} %collective-permute-done.9.msg_ref.other_ref, ...), custom_call_target="tpu_custom_call", output_to_operand_aliasing={{}: (5, {})} | custom-call | flops 2097152 | bytes 1572864 | tf_op jit(solution)/shard_map/merge/pallas_call | solution.py:226
  227.2 4.3 %merge.12.rest_0_ = bf16[512,3072]{1,0:T(8,128)(2,1)} custom-call(s32[4]{0:T(128)S(1)} %compare_convert_fusion.dead_ref, bf16[512,384]{1,0:T(8,128)(2,1)S(1)} %get-tuple-element.29.own_ref, f32[512,128]{1,0:T(8,128)S(1)} %get-tuple-element.30.stat_ref, bf16[512,512]{1,0:T(8,128)(2,1)S(1)} %collective-permute-done.6.msg_ref.other_ref, ...), custom_call_target="tpu_custom_call", output_to_operand_aliasing={{}: (5, {})} | custom-call | flops 1572864 | bytes 1179648 | tf_op jit(solution)/shard_map/merge/pallas_call | solution.py:226
  231.5 3.3 %merge.13 = bf16[512,3072]{1,0:T(8,128)(2,1)} custom-call(s32[4]{0:T(128)S(1)} %compare_convert_fusion.dead_ref, bf16[512,256]{1,0:T(8,128)(2,1)S(1)} %get-tuple-element.26.own_ref, f32[512,128]{1,0:T(8,128)S(1)} %get-tuple-element.27.stat_ref, bf16[512,384]{1,0:T(8,128)(2,1)S(1)} %collective-permute-done.3.msg_ref.other_ref, ...), custom_call_target="tpu_custom_call", output_to_operand_aliasing={{}: (5, {})} | custom-call | flops 1048576 | bytes 786432 | tf_op jit(solution)/shard_map/merge/pallas_call | solution.py:226
  (33 shorter events, 0.1 us)
Async XLA Ops:
  0.0 104.5 %collective-permute-start.1 = (bf16[2,512,3072]{2,1,0:T(8,128)(2,1)}, bf16[2,512,3072]{2,1,0:T(8,128)(2,1)}, u32[]{:S(2)}, u32[]{:S(2)}) collective-permute-start(bf16[2,512,3072]{2,1,0:T(8,128)(2,1)} %bitcast.3), channel_id=1, source_target_pairs={{0,1},{1,0},{2,3},{3,2},{4,5},{5,4},{6,7},{7,6},{8,9},{9,8},{10,11... | collective-permute-start | bytes 18874376 | tf_op jit(solution)/shard_map/ppermute | solution.py:171
  0.0 9.1 %copy-start = (bf16[2,1,512,3072]{3,2,1,0:T(8,128)(2,1)S(1)}, bf16[2,1,512,3072]{3,2,1,0:T(8,128)(2,1)}, u32[]{:S(2)}) copy-start(bf16[2,1,512,3072]{3,2,1,0:T(8,128)(2,1)} %param.5) | copy-start | bytes 18874372
  1.1 10.2 %collective-permute-start = (bf16[512,256]{1,0:T(8,128)(2,1)S(1)}, bf16[512,256]{1,0:T(8,128)(2,1)S(1)}, u32[]{:S(2)}, u32[]{:S(2)}) collective-permute-start(bf16[512,256]{1,0:T(8,128)(2,1)S(1)} %slice.56), channel_id=1, source_target_pairs={{0,16},{16,0},{1,17},{17,1},{2,18},{18,2},{3,19},{19,3},{4,20},{20... | collective-permute-start | bytes 786440 | tf_op jit(solution)/shard_map/ppermute | solution.py:179
  4.6 14.1 %collective-permute-start.19 = (bf16[512,384]{1,0:T(8,128)(2,1)S(1)}, bf16[512,384]{1,0:T(8,128)(2,1)S(1)}, u32[]{:S(2)}, u32[]{:S(2)}) collective-permute-start(bf16[512,384]{1,0:T(8,128)(2,1)S(1)} %get-tuple-element.53), channel_id=1, source_target_pairs={{0,16},{16,0},{1,17},{17,1},{2,18},{18,2},{3,19},{19,3},{4,20},{20... | collective-permute-start | bytes 1179656 | tf_op jit(solution)/shard_map/ppermute | solution.py:179
  7.8 22.2 %collective-permute-start.16 = (bf16[512,512]{1,0:T(8,128)(2,1)S(1)}, bf16[512,512]{1,0:T(8,128)(2,1)S(1)}, u32[]{:S(2)}, u32[]{:S(2)}) collective-permute-start(bf16[512,512]{1,0:T(8,128)(2,1)S(1)} %get-tuple-element.55), channel_id=1, source_target_pairs={{0,16},{16,0},{1,17},{17,1},{2,18},{18,2},{3,19},{19,3},{4,20},{20... | collective-permute-start | bytes 1572872 | tf_op jit(solution)/shard_map/ppermute | solution.py:179
  11.3 76.3 %copy-start.13 = (s32[4,8]{1,0:T(4,128)S(1)}, s32[4,8]{1,0:T(4,128)}, u32[]{:S(2)}) copy-start(s32[4,8]{1,0:T(4,128)} %param.6) | copy-start | bytes 388
  11.3 76.4 %copy-start.14 = (s32[4]{0:T(128)S(1)}, s32[4]{0:T(128)}, u32[]{:S(2)}) copy-start(s32[4]{0:T(128)} %param.7) | copy-start | bytes 52
  11.3 93.9 %copy-start.2 = (bf16[1,512,3072]{2,1,0:T(8,128)(2,1)S(1)}, bf16[1,512,3072]{2,1,0:T(8,128)(2,1)}, u32[]{:S(2)}) copy-start(bf16[1,512,3072]{2,1,0:T(8,128)(2,1)} %param.4) | copy-start | bytes 9437188
  11.3 76.3 %collective-permute-start.17 = (bf16[2,512,512]{2,1,0:T(8,128)(2,1)}, bf16[2,512,512]{2,1,0:T(8,128)(2,1)}, u32[]{:S(2)}, u32[]{:S(2)}) collective-permute-start(bf16[2,512,512]{2,1,0:T(8,128)(2,1)} %get-tuple-element.49), channel_id=1, source_target_pairs={{0,15},{1,2},{2,1},{3,4},{4,3},{5,6},{6,5},{7,8},{8,7},{9,10},{10,... | collective-permute-start | bytes 3145736 | tf_op jit(solution)/shard_map/ppermute | solution.py:178
  11.3 0.7 copy-start.9
  12.0 29.1 %collective-permute-start.13 = (bf16[512,512]{1,0:T(8,128)(2,1)S(1)}, bf16[512,512]{1,0:T(8,128)(2,1)S(1)}, u32[]{:S(2)}, u32[]{:S(2)}) collective-permute-start(bf16[512,512]{1,0:T(8,128)(2,1)S(1)} %get-tuple-element.56), channel_id=1, source_target_pairs={{0,16},{16,0},{1,17},{17,1},{2,18},{18,2},{3,19},{19,3},{4,20},{20... | collective-permute-start | bytes 1572872 | tf_op jit(solution)/shard_map/ppermute | solution.py:179
  18.7 33.3 %collective-permute-start.10 = (bf16[512,512]{1,0:T(8,128)(2,1)S(1)}, bf16[512,512]{1,0:T(8,128)(2,1)S(1)}, u32[]{:S(2)}, u32[]{:S(2)}) collective-permute-start(bf16[512,512]{1,0:T(8,128)(2,1)S(1)} %get-tuple-element.57), channel_id=1, source_target_pairs={{0,16},{16,0},{1,17},{17,1},{2,18},{18,2},{3,19},{19,3},{4,20},{20... | collective-permute-start | bytes 1572872 | tf_op jit(solution)/shard_map/ppermute | solution.py:179
  30.0 0.8 copy-start.5
  30.8 73.7 %collective-permute-start.14 = (bf16[2,512,512]{2,1,0:T(8,128)(2,1)}, bf16[2,512,512]{2,1,0:T(8,128)(2,1)}, u32[]{:S(2)}, u32[]{:S(2)}) collective-permute-start(bf16[2,512,512]{2,1,0:T(8,128)(2,1)} %get-tuple-element.50), channel_id=1, source_target_pairs={{0,15},{1,2},{2,1},{3,4},{4,3},{5,6},{6,5},{7,8},{8,7},{9,10},{10,... | collective-permute-start | bytes 3145736 | tf_op jit(solution)/shard_map/ppermute | solution.py:178
  41.2 0.8 copy-start.7
  42.0 107.8 %collective-permute-start.11 = (bf16[2,512,512]{2,1,0:T(8,128)(2,1)}, bf16[2,512,512]{2,1,0:T(8,128)(2,1)}, u32[]{:S(2)}, u32[]{:S(2)}) collective-permute-start(bf16[2,512,512]{2,1,0:T(8,128)(2,1)} %get-tuple-element.51), channel_id=1, source_target_pairs={{0,15},{1,2},{2,1},{3,4},{4,3},{5,6},{6,5},{7,8},{8,7},{9,10},{10,... | collective-permute-start | bytes 3145736 | tf_op jit(solution)/shard_map/ppermute | solution.py:178
  52.0 0.8 copy-start.3
  52.9 97.1 %collective-permute-start.8 = (bf16[2,512,512]{2,1,0:T(8,128)(2,1)}, bf16[2,512,512]{2,1,0:T(8,128)(2,1)}, u32[]{:S(2)}, u32[]{:S(2)}) collective-permute-start(bf16[2,512,512]{2,1,0:T(8,128)(2,1)} %get-tuple-element.52), channel_id=1, source_target_pairs={{0,15},{1,2},{2,1},{3,4},{4,3},{5,6},{6,5},{7,8},{8,7},{9,10},{10,... | collective-permute-start | bytes 3145736 | tf_op jit(solution)/shard_map/ppermute | solution.py:178
  87.6 47.7 %collective-permute-start.20 = (bf16[2,512,384]{2,1,0:T(8,128)(2,1)}, bf16[2,512,384]{2,1,0:T(8,128)(2,1)}, u32[]{:S(2)}, u32[]{:S(2)}) collective-permute-start(bf16[2,512,384]{2,1,0:T(8,128)(2,1)} %get-tuple-element.47), channel_id=1, source_target_pairs={{0,15},{1,2},{2,1},{3,4},{4,3},{5,6},{6,5},{7,8},{8,7},{9,10},{10,... | collective-permute-start | bytes 2359304 | tf_op jit(solution)/shard_map/ppermute | solution.py:178
  104.5 75.9 %collective-permute-start.5 = (bf16[2,512,384]{2,1,0:T(8,128)(2,1)}, bf16[2,512,384]{2,1,0:T(8,128)(2,1)S(1)}, u32[]{:S(2)}, u32[]{:S(2)}) collective-permute-start(bf16[2,512,384]{2,1,0:T(8,128)(2,1)} %get-tuple-element.48), channel_id=1, source_target_pairs={{0,15},{1,2},{2,1},{3,4},{4,3},{5,6},{6,5},{7,8},{8,7},{9,10},{10,... | collective-permute-start | bytes 2359304 | tf_op jit(solution)/shard_map/ppermute | solution.py:178
  104.5 39.7 %collective-permute-start.7 = (bf16[512,512]{1,0:T(8,128)(2,1)}, bf16[512,512]{1,0:T(8,128)(2,1)S(1)}, u32[]{:S(2)}, u32[]{:S(2)}) collective-permute-start(bf16[512,512]{1,0:T(8,128)(2,1)} %get-tuple-element.58), channel_id=1, source_target_pairs={{0,16},{16,0},{1,17},{17,1},{2,18},{18,2},{3,19},{19,3},{4,20},{20... | collective-permute-start | bytes 1572872 | tf_op jit(solution)/shard_map/ppermute | solution.py:179
  105.2 2.8 %copy-start.1 = (bf16[2,1,512,3072]{3,2,1,0:T(8,128)(2,1)S(1)}, bf16[2,1,512,3072]{3,2,1,0:T(8,128)(2,1)}, u32[]{:S(2)}) copy-start(bf16[2,1,512,3072]{3,2,1,0:T(8,128)(2,1)} %param.5) | copy-start | bytes 18874372
  108.0 1.0 copy-start.6
  109.0 11.1 %copy-start.8 = (bf16[512,512]{1,0:T(8,128)(2,1)S(1)}, bf16[512,512]{1,0:T(8,128)(2,1)}, u32[]{:S(2)}) copy-start(bf16[512,512]{1,0:T(8,128)(2,1)} %copy-done.7) | copy-start | bytes 1572868
  120.1 15.3 %copy-start.11 = (bf16[2,512,256]{2,1,0:T(8,128)(2,1)S(1)}, bf16[2,512,256]{2,1,0:T(8,128)(2,1)}, u32[]{:S(2)}) copy-start(bf16[2,512,256]{2,1,0:T(8,128)(2,1)} %slice.57) | copy-start | bytes 1572868
  131.2 13.0 %copy-start.12 = (bf16[512,384]{1,0:T(8,128)(2,1)S(1)}, bf16[512,384]{1,0:T(8,128)(2,1)}, u32[]{:S(2)}) copy-start(bf16[512,384]{1,0:T(8,128)(2,1)} %get-tuple-element.54) | copy-start | bytes 1179652
  131.2 20.7 %copy-start.4 = (bf16[512,512]{1,0:T(8,128)(2,1)S(1)}, bf16[512,512]{1,0:T(8,128)(2,1)}, u32[]{:S(2)}) copy-start(bf16[512,512]{1,0:T(8,128)(2,1)} %copy-done.3) | copy-start | bytes 1572868
  135.4 44.9 %collective-permute-start.2 = (bf16[2,512,256]{2,1,0:T(8,128)(2,1)S(1)}, bf16[2,512,256]{2,1,0:T(8,128)(2,1)S(1)}, u32[]{:S(2)}, u32[]{:S(2)}) collective-permute-start(bf16[2,512,256]{2,1,0:T(8,128)(2,1)S(1)} %copy-done.11), channel_id=1, source_target_pairs={{0,15},{1,2},{2,1},{3,4},{4,3},{5,6},{6,5},{7,8},{8,7},{9,10},{10,... | collective-permute-start | bytes 1572872 | tf_op jit(solution)/shard_map/ppermute | solution.py:178
  144.2 29.8 %collective-permute-start.4 = (bf16[512,384]{1,0:T(8,128)(2,1)S(1)}, bf16[512,384]{1,0:T(8,128)(2,1)S(1)}, u32[]{:S(2)}, u32[]{:S(2)}) collective-permute-start(bf16[512,384]{1,0:T(8,128)(2,1)S(1)} %copy-done.12), channel_id=1, source_target_pairs={{0,16},{16,0},{1,17},{17,1},{2,18},{18,2},{3,19},{19,3},{4,20},{20... | collective-permute-start | bytes 1179656 | tf_op jit(solution)/shard_map/ppermute | solution.py:179
  149.8 41.1 %collective-permute-start.21 = (bf16[512,512]{1,0:T(8,128)(2,1)S(1)}, bf16[512,512]{1,0:T(8,128)(2,1)S(1)}, u32[]{:S(2)}, u32[]{:S(2)}) collective-permute-start(bf16[512,512]{1,0:T(8,128)(2,1)S(1)} %get-tuple-element.46), channel_id=1, source_target_pairs={{0,16},{16,0},{1,17},{17,1},{2,18},{18,2},{3,19},{19,3},{4,20},{20... | collective-permute-start | bytes 1572872 | tf_op jit(solution)/shard_map/ppermute | solution.py:255
  149.9 49.7 %collective-permute-start.18 = (bf16[512,640]{1,0:T(8,128)(2,1)S(1)}, bf16[512,640]{1,0:T(8,128)(2,1)S(1)}, u32[]{:S(2)}, u32[]{:S(2)}) collective-permute-start(bf16[512,640]{1,0:T(8,128)(2,1)S(1)} %get-tuple-element.43), channel_id=1, source_target_pairs={{0,16},{16,0},{1,17},{17,1},{2,18},{18,2},{3,19},{19,3},{4,20},{20... | collective-permute-start | bytes 1966088 | tf_op jit(solution)/shard_map/ppermute | solution.py:255
  174.0 36.9 %collective-permute-start.15 = (bf16[512,640]{1,0:T(8,128)(2,1)S(1)}, bf16[512,640]{1,0:T(8,128)(2,1)S(1)}, u32[]{:S(2)}, u32[]{:S(2)}) collective-permute-start(bf16[512,640]{1,0:T(8,128)(2,1)S(1)} %get-tuple-element.40), channel_id=1, source_target_pairs={{0,16},{16,0},{1,17},{17,1},{2,18},{18,2},{3,19},{19,3},{4,20},{20... | collective-permute-start | bytes 1966088 | tf_op jit(solution)/shard_map/ppermute | solution.py:255
  180.3 35.9 %collective-permute-start.12 = (bf16[512,640]{1,0:T(8,128)(2,1)S(1)}, bf16[512,640]{1,0:T(8,128)(2,1)S(1)}, u32[]{:S(2)}, u32[]{:S(2)}) collective-permute-start(bf16[512,640]{1,0:T(8,128)(2,1)S(1)} %get-tuple-element.37), channel_id=1, source_target_pairs={{0,16},{16,0},{1,17},{17,1},{2,18},{18,2},{3,19},{19,3},{4,20},{20... | collective-permute-start | bytes 1966088 | tf_op jit(solution)/shard_map/ppermute | solution.py:255
  180.4 13.0 %copy-start.10 = (bf16[512,256]{1,0:T(8,128)(2,1)S(1)}, bf16[512,256]{1,0:T(8,128)(2,1)}, u32[]{:S(2)}) copy-start(bf16[512,256]{1,0:T(8,128)(2,1)} %copy-done.9) | copy-start | bytes 786436
  180.4 41.4 %collective-permute-start.9 = (bf16[512,640]{1,0:T(8,128)(2,1)S(1)}, bf16[512,640]{1,0:T(8,128)(2,1)S(1)}, u32[]{:S(2)}, u32[]{:S(2)}) collective-permute-start(bf16[512,640]{1,0:T(8,128)(2,1)S(1)} %get-tuple-element.34), channel_id=1, source_target_pairs={{0,16},{16,0},{1,17},{17,1},{2,18},{18,2},{3,19},{19,3},{4,20},{20... | collective-permute-start | bytes 1966088 | tf_op jit(solution)/shard_map/ppermute | solution.py:255
  191.0 36.2 %collective-permute-start.6 = (bf16[512,512]{1,0:T(8,128)(2,1)S(1)}, bf16[512,512]{1,0:T(8,128)(2,1)S(1)}, u32[]{:S(2)}, u32[]{:S(2)}) collective-permute-start(bf16[512,512]{1,0:T(8,128)(2,1)S(1)} %get-tuple-element.31), channel_id=1, source_target_pairs={{0,16},{16,0},{1,17},{17,1},{2,18},{18,2},{3,19},{19,3},{4,20},{20... | collective-permute-start | bytes 1572872 | tf_op jit(solution)/shard_map/ppermute | solution.py:255
  199.6 31.9 %collective-permute-start.3 = (bf16[512,384]{1,0:T(8,128)(2,1)S(1)}, bf16[512,384]{1,0:T(8,128)(2,1)S(1)}, u32[]{:S(2)}, u32[]{:S(2)}) collective-permute-start(bf16[512,384]{1,0:T(8,128)(2,1)S(1)} %get-tuple-element.28), channel_id=1, source_target_pairs={{0,16},{16,0},{1,17},{17,1},{2,18},{18,2},{3,19},{19,3},{4,20},{20... | collective-permute-start | bytes 1179656 | tf_op jit(solution)/shard_map/ppermute | solution.py:255

commit v2 on v1

v2 whole, which is shorter than its diff:
```python
import functools
import math

import jax
import jax.numpy as jnp
from jax import lax
from jax.experimental import pallas as pl
from jax.experimental.pallas import tpu as pltpu
from jax.sharding import PartitionSpec as P

HEAD = 128
TILE = 128
LOG2E = math.log2(math.e)
MASKED = -1e30 * LOG2E
LOWEST = -3e38
SPAN = 4
LANES = 16
SIZES = (4, 4, 4, 4, 4, 2, 1, 1)
DEPTH = 2
LAG = 2


def group_sizes(heads):
    if sum(SIZES) == heads:
        return SIZES
    return (4,) * (heads // 4) + (1,) * (heads % 4)


def parts_of(x):
    hi = x.astype(jnp.bfloat16).astype(jnp.float32)
    rest = x - hi
    mid = rest.astype(jnp.bfloat16).astype(jnp.float32)
    return hi, mid, rest - mid


def attend_kernel(
    slots_ref, dead_ref, q_ref, qp_ref, own_ref, even_ref, odd_ref,
    out_ref, stat_ref, msg_ref, windows, scores, sems,
    *, tiles, listed, heads, start, scale,
):
    head = pl.program_id(0)
    slot = head % 2
    columns = pl.ds(pl.multiple_of(head * HEAD, HEAD), HEAD)
    lane = lax.broadcasted_iota(jnp.int32, (TILE, HEAD), 1)
    own_row = lax.broadcasted_iota(jnp.int32, (2 * TILE, 1), 0) < TILE
    count = listed // SPAN
    wide = SPAN * TILE

    def copies(which):
        for region, ref in enumerate((own_ref, even_ref, odd_ref)):
            first = (which if region == 2 else start + which) * HEAD
            yield pltpu.make_async_copy(
                ref.at[:, :, :, pl.ds(pl.multiple_of(first, HEAD), HEAD)],
                windows.at[which % 2, :, region * tiles : (region + 1) * tiles],
                sems.at[which % 2, region],
            )

    @pl.when(head == 0)
    def _():
        for copy in copies(head):
            copy.start()
        stat_ref[...] = jnp.zeros_like(stat_ref)

    @pl.when(head + 1 < heads)
    def _():
        for copy in copies(head + 1):
            copy.start()

    for copy in copies(head):
        copy.wait()

    def rows_of(tile):
        return slice(tile * TILE, (tile + 1) * TILE)

    def gathered(kind, tile, index):
        first = tile * listed + SPAN * index
        return jnp.concatenate(
            [windows[slot, kind, slots_ref[first + k]] for k in range(SPAN)], 0
        )

    def score(tile, index, query, running):
        part = lax.dot_general(
            query, gathered(0, tile, index), (((1,), (1,)), ((), ())),
            preferred_element_type=jnp.float32,
        )
        scores[tile % 2, :, wide * index : wide * (index + 1)] = part
        for k in range(SPAN):
            piece = part[:, k * TILE : (k + 1) * TILE]
            running = piece if running is None else jnp.maximum(running, piece)
        return running

    def query_of(tile):
        return jnp.concatenate([q_ref[rows_of(tile), :], qp_ref[rows_of(tile), :]], 0)

    running = None
    query = query_of(0)
    for index in range(count):
        running = score(0, index, query, running)
    for tile in range(tiles):
        rows = rows_of(tile)
        floor = jnp.where(own_row & (dead_ref[tile] == 1), MASKED, LOWEST)
        top = jnp.maximum(jnp.max(running, axis=1, keepdims=True) * scale, floor)
        extra = jnp.where(floor == LOWEST, 0.0, jnp.exp2(floor - top))
        running, total, acc = None, None, None
        if tile + 1 < tiles:
            query = query_of(tile + 1)
        for index in range(count):
            if tile + 1 < tiles:
                running = score(tile + 1, index, query, running)
            part = scores[tile % 2, :, wide * index : wide * (index + 1)]
            weight = jnp.exp2(part * scale - top) + extra
            for k in range(SPAN):
                piece = weight[:, k * TILE : (k + 1) * TILE]
                total = piece if total is None else total + piece
            term = jnp.dot(
                weight.astype(jnp.bfloat16), gathered(1, tile, index),
                preferred_element_type=jnp.float32,
            )
            acc = term if acc is None else acc + term
        total = jnp.sum(total, axis=1, keepdims=True)
        result = (acc * (1.0 / total)).astype(jnp.bfloat16)
        out_ref[rows, :] = result[:TILE]
        msg_ref[rows, columns] = result[TILE:]
        stats = stat_ref[rows, :]
        for k, value in enumerate((top[:TILE], total[:TILE], top[TILE:], total[TILE:])):
            stats = jnp.where(lane == head + LANES * k, value, stats)
        stat_ref[rows, :] = stats

    @pl.when(head == heads - 1)
    def _():
        for tile in range(tiles):
            rows = rows_of(tile)
            packed = jnp.zeros((TILE, HEAD), jnp.float32)
            for k, value in enumerate(parts_of(stat_ref[rows, :])):
                moved = pltpu.roll(value, (HEAD - 2 * LANES + 2 * LANES * k) % HEAD, 1)
                packed = jnp.where(lane // (2 * LANES) == k, moved, packed)
            msg_ref[rows, heads * HEAD :] = packed.astype(jnp.bfloat16)


def merge_kernel(dead_ref, own_ref, stat_ref, msg_ref, *rest, heads):
    out_ref = rest[-1]
    dead = dead_ref[pl.program_id(0)]

    @pl.when(dead == 1)
    def _():
        out_ref[...] = own_ref[...]

    @pl.when(dead == 0)
    def _():
        mine = stat_ref[...]
        parts = msg_ref[:, heads * HEAD :].astype(jnp.float32)
        other = parts + pltpu.roll(parts, HEAD - 2 * LANES, 1)
        other = other + pltpu.roll(parts, HEAD - 4 * LANES, 1)
        most = jnp.maximum(mine, other)
        mine_w = pltpu.roll(mine, HEAD - LANES, 1) * jnp.exp2(mine - most)
        other_w = pltpu.roll(other, HEAD - LANES, 1) * jnp.exp2(other - most)
        inverse = 1.0 / (mine_w + other_w)
        mine_w, other_w = mine_w * inverse, other_w * inverse
        for head in range(heads):
            columns = slice(head * HEAD, (head + 1) * HEAD)
            result = own_ref[:, columns].astype(jnp.float32) * mine_w[:, head : head + 1]
            result = result + msg_ref[:, columns].astype(jnp.float32) * other_w[:, head : head + 1]
            out_ref[:, columns] = result.astype(out_ref.dtype)


def after(value, *done):
    return lax.optimization_barrier((value, *done))[0]


def local(queries, key_values, neighbours, clean_section):
    tok_dev, feat = queries.shape[1:]
    tiles = tok_dev // TILE
    listed = neighbours.shape[1]
    heads = feat // HEAD
    cycle = lax.axis_size("tile")
    here = lax.axis_index("tile")
    section = lax.axis_index("section")
    scale = HEAD ** (-0.5) * LOG2E

    query = queries[0]
    own = key_values[:, 0]
    dead = (clean_section == section).astype(jnp.int32)
    device = neighbours // tiles
    region = jnp.where(device == here, 0, jnp.where(device == here + 1 - 2 * (here % 2), 1, 2))
    slots = (region * tiles + neighbours % tiles).reshape(-1)

    even_pairs = [(i, i ^ 1) for i in range(cycle)]
    odd_pairs = [(i, (i + 1) % cycle if i % 2 else (i - 1) % cycle) for i in range(cycle)]
    swap = [(0, 1), (1, 0)]

    sizes = group_sizes(heads)
    starts = [sum(sizes[:g]) for g in range(len(sizes))]
    odd, partner = [], []
    even = None
    for g, (start, size) in enumerate(zip(starts, sizes)):
        low, high = start * HEAD, (start + size) * HEAD
        block, ask = own[:, :, low:high], query[:, low:high]
        if g >= DEPTH:
            block, odd[g - DEPTH] = lax.optimization_barrier((block, odd[g - DEPTH]))
            ask, partner[g - DEPTH] = lax.optimization_barrier((ask, partner[g - DEPTH]))
        odd.append(lax.ppermute(block, "tile", odd_pairs))
        partner.append(lax.ppermute(ask, "section", swap))
        if even is None:
            even = lax.ppermute(own, "tile", even_pairs)

    def rows4(x):
        return x.reshape(2, tiles, TILE, x.shape[-1])

    def attend(start, size, odd_part, partner_part, slots):
        units = size * tiles * 2 * TILE * listed * TILE
        return pl.pallas_call(
            functools.partial(
                attend_kernel, tiles=tiles, listed=listed, heads=size, start=start, scale=scale
            ),
            grid_spec=pltpu.PrefetchScalarGridSpec(
                num_scalar_prefetch=2,
                grid=(size,),
                in_specs=[
                    pl.BlockSpec((tok_dev, HEAD), lambda h, *_: (0, start + h)),
                    pl.BlockSpec((tok_dev, HEAD), lambda h, *_: (0, h)),
                ]
                + [pl.BlockSpec(memory_space=pl.ANY)] * 3,
                out_specs=[
                    pl.BlockSpec((tok_dev, HEAD), lambda h, *_: (0, h)),
                    pl.BlockSpec((tok_dev, HEAD), lambda h, *_: (0, 0)),
                    pl.BlockSpec((tok_dev, (size + 1) * HEAD), lambda h, *_: (0, 0)),
                ],
                scratch_shapes=[
                    pltpu.VMEM((2, 2, 3 * tiles, TILE, HEAD), jnp.bfloat16),
                    pltpu.VMEM((2, 2 * TILE, listed * TILE), jnp.float32),
                    pltpu.SemaphoreType.DMA((2, 3)),
                ],
            ),
            out_shape=[
                jax.ShapeDtypeStruct((tok_dev, size * HEAD), jnp.bfloat16),
                jax.ShapeDtypeStruct((tok_dev, HEAD), jnp.float32),
                jax.ShapeDtypeStruct((tok_dev, (size + 1) * HEAD), jnp.bfloat16),
            ],
            cost_estimate=pl.CostEstimate(
                flops=4 * units * HEAD, transcendentals=units,
                bytes_accessed=size * HEAD * tok_dev * 2 * 10,
            ),
            compiler_params=pltpu.CompilerParams(
                dimension_semantics=("arbitrary",), vmem_limit_bytes=24 << 20
            ),
            name="attend",
        )(slots, dead, query, partner_part, rows4(own), rows4(even), rows4(odd_part))

    def merge(start, size, mine, stats, message, target):
        last = [] if target is None else [target]
        return pl.pallas_call(
            functools.partial(merge_kernel, heads=size),
            grid_spec=pltpu.PrefetchScalarGridSpec(
                num_scalar_prefetch=1,
                grid=(tiles,),
                in_specs=[
                    pl.BlockSpec((TILE, size * HEAD), lambda t, *_: (t, 0)),
                    pl.BlockSpec((TILE, HEAD), lambda t, *_: (t, 0)),
                    pl.BlockSpec((TILE, (size + 1) * HEAD), lambda t, *_: (t, 0)),
                ]
                + [pl.BlockSpec(memory_space=pl.ANY)] * len(last),
                out_specs=pl.BlockSpec((TILE, size * HEAD), lambda t, *_: (t, start // size)),
            ),
            out_shape=jax.ShapeDtypeStruct((tok_dev, feat), jnp.bfloat16),
            input_output_aliases={4: 0} if last else {},
            cost_estimate=pl.CostEstimate(
                flops=size * HEAD * tok_dev * 8, transcendentals=0,
                bytes_accessed=size * HEAD * tok_dev * 2 * 3,
            ),
            compiler_params=pltpu.CompilerParams(
                dimension_semantics=("arbitrary",), vmem_limit_bytes=16 << 20
            ),
            name="merge",
        )(dead, mine, stats, message, *last)

    target = None
    waiting = []
    for g, (start, size) in enumerate(zip(starts, sizes)):
        index = slots
        if len(waiting) >= LAG:
            target = merge(*waiting.pop(0), target)
            index, target = lax.optimization_barrier((slots, target))
        mine, stats, message = attend(start, size, odd[g], partner[g], index)
        waiting.append((start, size, mine, stats, lax.ppermute(message, "section", swap)))
    for item in waiting:
        target = merge(*item, target)
    return target[None]


def solution(mesh):
    placed = (
        P("section", "tile", None),
        P(None, "section", "tile", None),
        P("tile", None),
        P("tile"),
    )
    return jax.shard_map(
        local, mesh=mesh, in_specs=placed, out_specs=P("section", "tile", None), check_vma=False
    )
```

time: 231 us -> 212 us (0.918); the launches traced: 235 us -> 210 us
  Pallas kernels: 101 us -> 79.6 us
  waiting for transfers between devices: 88.7 us -> 101 us
  local copies, waits for them, and re-layouts: 18 us -> 9.71 us
  starting transfers between devices: 26.8 us -> 20 us
    pallas_call x7 -> x8, Pallas kernels: 33.5 us -> 20.4 us  [merge(): pl.pallas_call(functools.partial(merge_kernel, heads=size), grid_spec=plt...]
    ppermute x21 -> x24, waiting for transfers between devices: 88.7 us -> 101 us  [the longest x8 71.1 us: local(): odd.append(lax.ppermute(block, 'tile', odd_pairs))]
    pallas_call x7 -> x8, Pallas kernels: 67.6 us -> 59.2 us  [attend(): pl.pallas_call(functools.partial(attend_kernel, tiles=tiles, listed=liste...]
    ppermute x21 -> x24, starting transfers between devices: 26.8 us -> 20 us  [the longest x8 9.56 us: local(): partner.append(lax.ppermute(ask, 'section', swap))]
    unnamed x30 -> x20, local copies, waits for them, and re-layouts: 7.02 us -> 2.82 us
    slice x6, local copies, waits for them, and re-layouts: 10.9 us -> 6.81 us  [local(): block, ask = (own[:, :, low:high], query[:, low:high])]
  transfers between devices with their start and end apart: 22 -> 25, of which waited for: 7 -> 7; matrix products, arithmetic and copies ran while one was open for 5% -> 3% of each run, Pallas kernels for 42% -> 37%
where the time goes in v2:
time: 212 us; the launch traced here: 210 us
  waiting for transfers between devices  101 us (48%)
  Pallas kernels  79.6 us (38%)
  starting transfers between devices  20 us (9%)
  local copies, waits for them, and re-layouts  9.71 us (5%)
    ppermute x8, waiting for transfers between devices, local(): odd.append(lax.ppermute(block, 'tile', odd_pairs))  71.1 us
    pallas_call x8, Pallas kernels, attend(): pl.pallas_call(functools.partial(attend_kernel, tiles=tiles, listed=liste...  59.2 us
    pallas_call x8, Pallas kernels, merge(): pl.pallas_call(functools.partial(merge_kernel, heads=size), grid_spec=plt...  20.4 us
    ppermute x8, waiting for transfers between devices, local(): lax.ppermute(message, 'section', swap)  15.5 us
    ppermute x8, waiting for transfers between devices, local(): partner.append(lax.ppermute(ask, 'section', swap))  14 us
    ppermute x8, starting transfers between devices, local(): partner.append(lax.ppermute(ask, 'section', swap))  9.56 us
    slice x6, local copies, waits for them, and re-layouts, local(): block, ask = (own[:, :, low:high], query[:, low:high])  6.81 us
    ppermute x8, starting transfers between devices, local(): odd.append(lax.ppermute(block, 'tile', odd_pairs))  5.54 us
  transfers between devices with their start and end apart: 25, of which 7 were waited for; matrix products, arithmetic and copies ran while one was open for 3% of the time, Pallas kernels for 37%

profile of v2, /device:TPU:12, one launch (start us, length us, event | category | flops | bytes accessed | tf_op | source)
XLA Modules:
  0.0 210.2 jit_solution(16158207969044912611)
XLA Ops:
  0.0 0.0 collective-permute-start.1
  0.0 5.1 %fusion.3 = (bf16[2,512,512]{2,1,0:T(8,128)(2,1)}, bf16[2,512,512]{2,1,0:T(8,128)(2,1)}, bf16[2,512,512]{2,1,0:T(8,128)(2,1)}, bf16[2,512,512]{2,1,0:T(8,128)(2,1)}, bf16[2,512,512]{2,1,0:T(8,128)(2,1)}) fusion(bf16[2,512,3072]{2,1,0:T(8,128)(2,1)} %bitcast.14), kind=kLoop, calls=%fused_computation.10 | loop fusion | bytes 10485760 | tf_op jit(solution)/shard_map/slice | solution.py:197
  5.1 0.7 collective-permute-start.5
  5.8 1.0 collective-permute-start.2
  6.9 1.5 fusion.5
  8.3 1.5 collective-permute-start.4
  9.8 0.5 collective-permute-start
  10.4 71.1 %collective-permute-done.5 = bf16[2,512,512]{2,1,0:T(8,128)(2,1)} collective-permute-done((bf16[2,512,512]{2,1,0:T(8,128)(2,1)}, bf16[2,512,512]{2,1,0:T(8,128)(2,1)}, u32[]{:S(2)}, u32[]{:S(2)}) %collective-permute-start.5) | collective-permute-done | bytes 1048608 | tf_op jit(solution)/shard_map/ppermute | solution.py:201
  81.4 0.7 collective-permute-start.11
  82.2 0.1 reshape.37.slots_ref
  82.3 0.0 collective-permute-done.4.qp_ref
  82.3 1.5 collective-permute-start.10
  83.8 0.0 collective-permute-done.1
  83.8 2.8 %copy-done = bf16[2,1,512,3072]{3,2,1,0:T(8,128)(2,1)S(1)} copy-done((bf16[2,1,512,3072]{3,2,1,0:T(8,128)(2,1)S(1)}, bf16[2,1,512,3072]{3,2,1,0:T(8,128)(2,1)}, u32[]{:S(2)}) %copy-start) | copy-done | bytes 6291480
  86.6 9.8 %attend.9 = (bf16[512,512]{1,0:T(8,128)(2,1)S(1)}, f32[512,128]{1,0:T(8,128)S(1)}, bf16[512,640]{1,0:T(8,128)(2,1)S(1)}) custom-call(s32[32]{0:T(128)S(1)} %reshape.37.slots_ref, s32[4]{0:T(128)S(1)} %compare_convert_fusion.dead_ref, bf16[512,3072]{1,0:T(8,128)(2,1)S(1)} %bitcast.28, bf16[512,512]{1,0:T(8,128)(2,1)} %collective-permute-done.4.qp_ref, ...), custom_call_target="tpu_custom_call" | custom-call | flops 2147483648 | bytes 5242880 | tf_op jit(solution)/shard_map/attend/pallas_call | solution.py:211
  96.4 0.6 collective-permute-start.6
  97.0 0.0 collective-permute-done.2
  97.0 0.5 collective-permute-start.8
  97.5 1.5 collective-permute-start.7
  99.0 9.8 %attend.8 = (bf16[512,512]{1,0:T(8,128)(2,1)S(1)}, f32[512,128]{1,0:T(8,128)S(1)}, bf16[512,640]{1,0:T(8,128)(2,1)S(1)}) custom-call(s32[32]{0:T(128)S(1)} %reshape.37.slots_ref, s32[4]{0:T(128)S(1)} %compare_convert_fusion.dead_ref, bf16[512,3072]{1,0:T(8,128)(2,1)S(1)} %bitcast.29, bf16[512,512]{1,0:T(8,128)(2,1)} %collective-permute-done.qp_ref, ...), custom_call_target="tpu_custom_call" | custom-call | flops 2147483648 | bytes 5242880 | tf_op jit(solution)/shard_map/attend/pallas_call | solution.py:211
  108.8 0.6 collective-permute-start.3
  109.4 0.0 collective-permute-done.10.qp_ref
  109.4 0.7 collective-permute-start.17
  110.2 3.3 %collective-permute-done.6.msg_ref = bf16[512,640]{1,0:T(8,128)(2,1)S(1)} collective-permute-done((bf16[512,640]{1,0:T(8,128)(2,1)S(1)}, bf16[512,640]{1,0:T(8,128)(2,1)S(1)}, u32[]{:S(2)}, u32[]{:S(2)}) %collective-permute-start.6) | collective-permute-done | bytes 655392 | tf_op jit(solution)/shard_map/ppermute | solution.py:284
  113.4 0.5 collective-permute-start.16
  113.9 2.7 %merge.8.rest_0_ = bf16[512,3072]{1,0:T(8,128)(2,1)} custom-call(s32[4]{0:T(128)S(1)} %compare_convert_fusion.dead_ref, bf16[512,512]{1,0:T(8,128)(2,1)S(1)} %get-tuple-element.72.own_ref, f32[512,128]{1,0:T(8,128)S(1)} %get-tuple-element.73.stat_ref, bf16[512,640]{1,0:T(8,128)(2,1)S(1)} %collective-permute-done.6.msg_ref), custom_call_target="tpu_custom_call" | custom-call | flops 2097152 | bytes 1572864 | tf_op jit(solution)/shard_map/merge/pallas_call | solution.py:251
  116.6 9.1 %attend.11 = (bf16[512,512]{1,0:T(8,128)(2,1)S(1)}, f32[512,128]{1,0:T(8,128)S(1)}, bf16[512,640]{1,0:T(8,128)(2,1)S(1)}) custom-call(s32[32]{0:T(128)S(1)} %reshape.37.slots_ref, s32[4]{0:T(128)S(1)} %compare_convert_fusion.dead_ref, bf16[512,3072]{1,0:T(8,128)(2,1)S(1)} %bitcast.30, bf16[512,512]{1,0:T(8,128)(2,1)S(1)} %collective-permute-done.10.qp_ref, ...), custom_call_target="tpu_custom_call" | custom-call | flops 2147483648 | bytes 5242880 | tf_op jit(solution)/shard_map/attend/pallas_call | solution.py:211
  125.7 0.0 collective-permute-done.7.qp_ref
  125.7 1.2 collective-permute-start.12
  126.9 0.1 fusion.2
  127.0 0.1 slice.73
  127.1 0.0 collective-permute-done.8
  127.1 0.1 collective-permute-start.14
  127.2 1.0 collective-permute-done.3.msg_ref
  128.3 2.7 %merge.9.rest_0_ = bf16[512,3072]{1,0:T(8,128)(2,1)} custom-call(s32[4]{0:T(128)S(1)} %compare_convert_fusion.dead_ref, bf16[512,512]{1,0:T(8,128)(2,1)S(1)} %get-tuple-element.67.own_ref, f32[512,128]{1,0:T(8,128)S(1)} %get-tuple-element.68.stat_ref, bf16[512,640]{1,0:T(8,128)(2,1)S(1)} %collective-permute-done.3.msg_ref, ...), custom_call_target="tpu_custom_call", output_to_operand_aliasing={{}: (4, {})} | custom-call | flops 2097152 | bytes 1572864 | tf_op jit(solution)/shard_map/merge/pallas_call | solution.py:251
  130.9 9.1 %attend.10 = (bf16[512,512]{1,0:T(8,128)(2,1)S(1)}, f32[512,128]{1,0:T(8,128)S(1)}, bf16[512,640]{1,0:T(8,128)(2,1)S(1)}) custom-call(s32[32]{0:T(128)S(1)} %reshape.37.slots_ref, s32[4]{0:T(128)S(1)} %compare_convert_fusion.dead_ref, bf16[512,3072]{1,0:T(8,128)(2,1)S(1)} %bitcast.32, bf16[512,512]{1,0:T(8,128)(2,1)S(1)} %collective-permute-done.7.qp_ref, ...), custom_call_target="tpu_custom_call" | custom-call | flops 2147483648 | bytes 5242880 | tf_op jit(solution)/shard_map/attend/pallas_call | solution.py:211
  140.0 0.4 collective-permute-start.9
  140.5 0.0 collective-permute-done.16.qp_ref
  140.5 8.9 %collective-permute-done.12.msg_ref = bf16[512,640]{1,0:T(8,128)(2,1)S(1)} collective-permute-done((bf16[512,640]{1,0:T(8,128)(2,1)S(1)}, bf16[512,640]{1,0:T(8,128)(2,1)S(1)}, u32[]{:S(2)}, u32[]{:S(2)}) %collective-permute-start.12) | collective-permute-done | bytes 655392 | tf_op jit(solution)/shard_map/ppermute | solution.py:284
  149.4 2.7 %merge.10.rest_0_ = bf16[512,3072]{1,0:T(8,128)(2,1)} custom-call(s32[4]{0:T(128)S(1)} %compare_convert_fusion.dead_ref, bf16[512,512]{1,0:T(8,128)(2,1)S(1)} %get-tuple-element.89.own_ref, f32[512,128]{1,0:T(8,128)S(1)} %get-tuple-element.90.stat_ref, bf16[512,640]{1,0:T(8,128)(2,1)S(1)} %collective-permute-done.12.msg_ref, ...), custom_call_target="tpu_custom_call", output_to_operand_aliasing={{}: (4, {})} | custom-call | flops 2097152 | bytes 1572864 | tf_op jit(solution)/shard_map/merge/pallas_call | solution.py:251
  152.1 9.3 %attend.13 = (bf16[512,512]{1,0:T(8,128)(2,1)S(1)}, f32[512,128]{1,0:T(8,128)S(1)}, bf16[512,640]{1,0:T(8,128)(2,1)S(1)}) custom-call(s32[32]{0:T(128)S(1)} %reshape.37.slots_ref, s32[4]{0:T(128)S(1)} %compare_convert_fusion.dead_ref, bf16[512,3072]{1,0:T(8,128)(2,1)S(1)} %bitcast.34, bf16[512,512]{1,0:T(8,128)(2,1)S(1)} %collective-permute-done.16.qp_ref, ...), custom_call_target="tpu_custom_call" | custom-call | flops 2147483648 | bytes 5242880 | tf_op jit(solution)/shard_map/attend/pallas_call | solution.py:211
  161.3 0.1 collective-permute-start.18
  161.4 2.0 collective-permute-start.13
  163.4 11.4 %collective-permute-done.13.qp_ref = bf16[512,256]{1,0:T(8,128)(2,1)S(1)} collective-permute-done((bf16[512,256]{1,0:T(8,128)(2,1)S(1)}, bf16[512,256]{1,0:T(8,128)(2,1)S(1)}, u32[]{:S(2)}, u32[]{:S(2)}) %collective-permute-start.13) | collective-permute-done | bytes 262176 | tf_op jit(solution)/shard_map/ppermute | solution.py:202
  174.8 0.0 collective-permute-done.9.msg_ref
  174.8 2.7 %merge.11.rest_0_ = bf16[512,3072]{1,0:T(8,128)(2,1)} custom-call(s32[4]{0:T(128)S(1)} %compare_convert_fusion.dead_ref, bf16[512,512]{1,0:T(8,128)(2,1)S(1)} %get-tuple-element.81.own_ref, f32[512,128]{1,0:T(8,128)S(1)} %get-tuple-element.82.stat_ref, bf16[512,640]{1,0:T(8,128)(2,1)S(1)} %collective-permute-done.9.msg_ref, ...), custom_call_target="tpu_custom_call", output_to_operand_aliasing={{}: (4, {})} | custom-call | flops 2097152 | bytes 1572864 | tf_op jit(solution)/shard_map/merge/pallas_call | solution.py:251
  177.5 5.3 %attend.12 = (bf16[512,256]{1,0:T(8,128)(2,1)S(1)}, f32[512,128]{1,0:T(8,128)S(1)}, bf16[512,384]{1,0:T(8,128)(2,1)S(1)}) custom-call(s32[32]{0:T(128)S(1)} %reshape.37.slots_ref, s32[4]{0:T(128)S(1)} %compare_convert_fusion.dead_ref, bf16[512,3072]{1,0:T(8,128)(2,1)S(1)} %bitcast.35, bf16[512,256]{1,0:T(8,128)(2,1)S(1)} %collective-permute-done.13.qp_ref, ...), custom_call_target="tpu_custom_call" | custom-call | flops 1073741824 | bytes 2621440 | tf_op jit(solution)/shard_map/attend/pallas_call | solution.py:211
  182.8 0.1 collective-permute-start.15
  182.9 0.1 collective-permute-start.23
  182.9 1.7 collective-permute-start.20
  184.7 1.9 collective-permute-start.22
  186.6 0.0 collective-permute-done.18.msg_ref
  186.6 0.1 collective-permute-start.19
  186.7 2.7 %merge.12.rest_0_ = bf16[512,3072]{1,0:T(8,128)(2,1)} custom-call(s32[4]{0:T(128)S(1)} %compare_convert_fusion.dead_ref, bf16[512,512]{1,0:T(8,128)(2,1)S(1)} %get-tuple-element.107.own_ref, f32[512,128]{1,0:T(8,128)S(1)} %get-tuple-element.108.stat_ref, bf16[512,640]{1,0:T(8,128)(2,1)S(1)} %collective-permute-done.18.msg_ref, ...), custom_call_target="tpu_custom_call", output_to_operand_aliasing={{}: (4, {})} | custom-call | flops 2097152 | bytes 1572864 | tf_op jit(solution)/shard_map/merge/pallas_call | solution.py:251
  189.4 2.7 %collective-permute-done.22.qp_ref = bf16[512,128]{1,0:T(8,128)(2,1)S(1)} collective-permute-done((bf16[512,128]{1,0:T(8,128)(2,1)S(1)}, bf16[512,128]{1,0:T(8,128)(2,1)S(1)}, u32[]{:S(2)}, u32[]{:S(2)}) %collective-permute-start.22) | collective-permute-done | bytes 131104 | tf_op jit(solution)/shard_map/ppermute | solution.py:202
  192.0 3.4 %attend.15 = (bf16[512,128]{1,0:T(8,128)(2,1)S(1)}, f32[512,128]{1,0:T(8,128)S(1)}, bf16[512,256]{1,0:T(8,128)(2,1)S(1)}) custom-call(s32[32]{0:T(128)S(1)} %reshape.37.slots_ref, s32[4]{0:T(128)S(1)} %compare_convert_fusion.dead_ref, bf16[512,3072]{1,0:T(8,128)(2,1)S(1)} %bitcast.36, bf16[512,128]{1,0:T(8,128)(2,1)S(1)} %collective-permute-done.22.qp_ref, ...), custom_call_target="tpu_custom_call" | custom-call | flops 536870912 | bytes 1310720 | tf_op jit(solution)/shard_map/attend/pallas_call | solution.py:211
  195.5 0.1 collective-permute-start.24
  195.6 2.4 %merge.13.rest_0_ = bf16[512,3072]{1,0:T(8,128)(2,1)} custom-call(s32[4]{0:T(128)S(1)} %compare_convert_fusion.dead_ref, bf16[512,256]{1,0:T(8,128)(2,1)S(1)} %get-tuple-element.99.own_ref, f32[512,128]{1,0:T(8,128)S(1)} %get-tuple-element.100.stat_ref, bf16[512,384]{1,0:T(8,128)(2,1)S(1)} %collective-permute-done.15.msg_ref, ...), custom_call_target="tpu_custom_call", output_to_operand_aliasing={{}: (4, {})} | custom-call | flops 1048576 | bytes 786432 | tf_op jit(solution)/shard_map/merge/pallas_call | solution.py:251
  198.0 3.4 %attend.14 = (bf16[512,128]{1,0:T(8,128)(2,1)S(1)}, f32[512,128]{1,0:T(8,128)S(1)}, bf16[512,256]{1,0:T(8,128)(2,1)S(1)}) custom-call(s32[32]{0:T(128)S(1)} %reshape.37.slots_ref, s32[4]{0:T(128)S(1)} %compare_convert_fusion.dead_ref, bf16[512,3072]{1,0:T(8,128)(2,1)S(1)} %bitcast.37, bf16[512,128]{1,0:T(8,128)(2,1)S(1)} %collective-permute-done.19.qp_ref, ...), custom_call_target="tpu_custom_call" | custom-call | flops 536870912 | bytes 1310720 | tf_op jit(solution)/shard_map/attend/pallas_call | solution.py:211
  201.5 1.8 collective-permute-start.21
  203.2 0.0 collective-permute-done.24.msg_ref
  203.2 2.3 %merge.14.rest_0_ = bf16[512,3072]{1,0:T(8,128)(2,1)} custom-call(s32[4]{0:T(128)S(1)} %compare_convert_fusion.dead_ref, bf16[512,128]{1,0:T(8,128)(2,1)S(1)} %get-tuple-element.121.own_ref, f32[512,128]{1,0:T(8,128)S(1)} %get-tuple-element.122.stat_ref, bf16[512,256]{1,0:T(8,128)(2,1)S(1)} %collective-permute-done.24.msg_ref, ...), custom_call_target="tpu_custom_call", output_to_operand_aliasing={{}: (4, {})} | custom-call | flops 524288 | bytes 393216 | tf_op jit(solution)/shard_map/merge/pallas_call | solution.py:251
  205.6 2.3 %collective-permute-done.21.msg_ref = bf16[512,256]{1,0:T(8,128)(2,1)S(1)} collective-permute-done((bf16[512,256]{1,0:T(8,128)(2,1)S(1)}, bf16[512,256]{1,0:T(8,128)(2,1)S(1)}, u32[]{:S(2)}, u32[]{:S(2)}) %collective-permute-start.21) | collective-permute-done | bytes 262176 | tf_op jit(solution)/shard_map/ppermute | solution.py:284
  207.9 2.3 %merge.15 = bf16[512,3072]{1,0:T(8,128)(2,1)} custom-call(s32[4]{0:T(128)S(1)} %compare_convert_fusion.dead_ref, bf16[512,128]{1,0:T(8,128)(2,1)S(1)} %get-tuple-element.115.own_ref, f32[512,128]{1,0:T(8,128)S(1)} %get-tuple-element.116.stat_ref, bf16[512,256]{1,0:T(8,128)(2,1)S(1)} %collective-permute-done.21.msg_ref, ...), custom_call_target="tpu_custom_call", output_to_operand_aliasing={{}: (4, {})} | custom-call | flops 524288 | bytes 393216 | tf_op jit(solution)/shard_map/merge/pallas_call | solution.py:251
  (32 shorter events, 0.1 us)
Async XLA Ops:
  0.0 6.9 %copy-start.1 = (bf16[1,512,3072]{2,1,0:T(8,128)(2,1)S(1)}, bf16[1,512,3072]{2,1,0:T(8,128)(2,1)}, u32[]{:S(2)}) copy-start(bf16[1,512,3072]{2,1,0:T(8,128)(2,1)} %param.4) | copy-start | bytes 9437188
  0.0 83.8 %collective-permute-start.1 = (bf16[2,512,3072]{2,1,0:T(8,128)(2,1)}, bf16[2,512,3072]{2,1,0:T(8,128)(2,1)}, u32[]{:S(2)}, u32[]{:S(2)}) collective-permute-start(bf16[2,512,3072]{2,1,0:T(8,128)(2,1)} %bitcast.13), channel_id=1, source_target_pairs={{0,1},{1,0},{2,3},{3,2},{4,5},{5,4},{6,7},{7,6},{8,9},{9,8},{10,11... | collective-permute-start | bytes 18874376 | tf_op jit(solution)/shard_map/ppermute | solution.py:204
  5.1 77.1 %copy-start.6 = (s32[4,8]{1,0:T(4,128)S(1)}, s32[4,8]{1,0:T(4,128)}, u32[]{:S(2)}) copy-start(s32[4,8]{1,0:T(4,128)} %param.6) | copy-start | bytes 388
  5.1 77.1 %copy-start.7 = (s32[4]{0:T(128)S(1)}, s32[4]{0:T(128)}, u32[]{:S(2)}) copy-start(s32[4]{0:T(128)} %param.7) | copy-start | bytes 52
  5.1 76.3 %collective-permute-start.5 = (bf16[2,512,512]{2,1,0:T(8,128)(2,1)}, bf16[2,512,512]{2,1,0:T(8,128)(2,1)}, u32[]{:S(2)}, u32[]{:S(2)}) collective-permute-start(bf16[2,512,512]{2,1,0:T(8,128)(2,1)} %get-tuple-element.128), channel_id=1, source_target_pairs={{0,15},{1,2},{2,1},{3,4},{4,3},{5,6},{6,5},{7,8},{8,7},{9,10},{10,... | collective-permute-start | bytes 3145736 | tf_op jit(solution)/shard_map/ppermute | solution.py:201
  5.8 91.2 %collective-permute-start.2 = (bf16[2,512,512]{2,1,0:T(8,128)(2,1)}, bf16[2,512,512]{2,1,0:T(8,128)(2,1)}, u32[]{:S(2)}, u32[]{:S(2)}) collective-permute-start(bf16[2,512,512]{2,1,0:T(8,128)(2,1)} %get-tuple-element.130), channel_id=1, source_target_pairs={{0,15},{1,2},{2,1},{3,4},{4,3},{5,6},{6,5},{7,8},{8,7},{9,10},{10,... | collective-permute-start | bytes 3145736 | tf_op jit(solution)/shard_map/ppermute | solution.py:201
  8.3 74.0 %collective-permute-start.4 = (bf16[512,512]{1,0:T(8,128)(2,1)}, bf16[512,512]{1,0:T(8,128)(2,1)}, u32[]{:S(2)}, u32[]{:S(2)}) collective-permute-start(bf16[512,512]{1,0:T(8,128)(2,1)} %get-tuple-element.135), channel_id=1, source_target_pairs={{0,16},{16,0},{1,17},{17,1},{2,18},{18,2},{3,19},{19,3},{4,20},{20... | collective-permute-start | bytes 1572872 | tf_op jit(solution)/shard_map/ppermute | solution.py:202
  9.8 87.6 %collective-permute-start = (bf16[512,512]{1,0:T(8,128)(2,1)}, bf16[512,512]{1,0:T(8,128)(2,1)}, u32[]{:S(2)}, u32[]{:S(2)}) collective-permute-start(bf16[512,512]{1,0:T(8,128)(2,1)} %get-tuple-element.137), channel_id=1, source_target_pairs={{0,16},{16,0},{1,17},{17,1},{2,18},{18,2},{3,19},{19,3},{4,20},{20... | collective-permute-start | bytes 1572872 | tf_op jit(solution)/shard_map/ppermute | solution.py:202
  81.4 27.4 %collective-permute-start.11 = (bf16[2,512,512]{2,1,0:T(8,128)(2,1)}, bf16[2,512,512]{2,1,0:T(8,128)(2,1)}, u32[]{:S(2)}, u32[]{:S(2)}) collective-permute-start(bf16[2,512,512]{2,1,0:T(8,128)(2,1)} %get-tuple-element.87), channel_id=1, source_target_pairs={{0,15},{1,2},{2,1},{3,4},{4,3},{5,6},{6,5},{7,8},{8,7},{9,10},{10,... | collective-permute-start | bytes 3145736 | tf_op jit(solution)/shard_map/ppermute | solution.py:201
  82.3 27.1 %collective-permute-start.10 = (bf16[512,512]{1,0:T(8,128)(2,1)}, bf16[512,512]{1,0:T(8,128)(2,1)S(1)}, u32[]{:S(2)}, u32[]{:S(2)}) collective-permute-start(bf16[512,512]{1,0:T(8,128)(2,1)} %get-tuple-element.85), channel_id=1, source_target_pairs={{0,16},{16,0},{1,17},{17,1},{2,18},{18,2},{3,19},{19,3},{4,20},{20... | collective-permute-start | bytes 1572872 | tf_op jit(solution)/shard_map/ppermute | solution.py:202
  83.8 2.8 %copy-start = (bf16[2,1,512,3072]{3,2,1,0:T(8,128)(2,1)S(1)}, bf16[2,1,512,3072]{3,2,1,0:T(8,128)(2,1)}, u32[]{:S(2)}) copy-start(bf16[2,1,512,3072]{3,2,1,0:T(8,128)(2,1)} %param.5) | copy-start | bytes 18874372
  86.6 10.4 %copy-start.3 = (bf16[2,512,512]{2,1,0:T(8,128)(2,1)S(1)}, bf16[2,512,512]{2,1,0:T(8,128)(2,1)}, u32[]{:S(2)}) copy-start(bf16[2,512,512]{2,1,0:T(8,128)(2,1)} %get-tuple-element.79) | copy-start | bytes 3145732
  86.6 10.9 %copy-start.5 = (bf16[512,512]{1,0:T(8,128)(2,1)S(1)}, bf16[512,512]{1,0:T(8,128)(2,1)}, u32[]{:S(2)}) copy-start(bf16[512,512]{1,0:T(8,128)(2,1)} %get-tuple-element.77) | copy-start | bytes 1572868
  96.4 17.0 %collective-permute-start.6 = (bf16[512,640]{1,0:T(8,128)(2,1)S(1)}, bf16[512,640]{1,0:T(8,128)(2,1)S(1)}, u32[]{:S(2)}, u32[]{:S(2)}) collective-permute-start(bf16[512,640]{1,0:T(8,128)(2,1)S(1)} %get-tuple-element.74), channel_id=1, source_target_pairs={{0,16},{16,0},{1,17},{17,1},{2,18},{18,2},{3,19},{19,3},{4,20},{20... | collective-permute-start | bytes 1966088 | tf_op jit(solution)/shard_map/ppermute | solution.py:284
  97.0 30.1 %collective-permute-start.8 = (bf16[2,512,512]{2,1,0:T(8,128)(2,1)S(1)}, bf16[2,512,512]{2,1,0:T(8,128)(2,1)S(1)}, u32[]{:S(2)}, u32[]{:S(2)}) collective-permute-start(bf16[2,512,512]{2,1,0:T(8,128)(2,1)S(1)} %copy-done.3), channel_id=1, source_target_pairs={{0,15},{1,2},{2,1},{3,4},{4,3},{5,6},{6,5},{7,8},{8,7},{9,10},{10,... | collective-permute-start | bytes 3145736 | tf_op jit(solution)/shard_map/ppermute | solution.py:201
  97.5 28.2 %collective-permute-start.7 = (bf16[512,512]{1,0:T(8,128)(2,1)S(1)}, bf16[512,512]{1,0:T(8,128)(2,1)S(1)}, u32[]{:S(2)}, u32[]{:S(2)}) collective-permute-start(bf16[512,512]{1,0:T(8,128)(2,1)S(1)} %copy-done.5), channel_id=1, source_target_pairs={{0,16},{16,0},{1,17},{17,1},{2,18},{18,2},{3,19},{19,3},{4,20},{20... | collective-permute-start | bytes 1572872 | tf_op jit(solution)/shard_map/ppermute | solution.py:202
  99.0 10.5 %copy-start.2 = (bf16[2,512,512]{2,1,0:T(8,128)(2,1)S(1)}, bf16[2,512,512]{2,1,0:T(8,128)(2,1)}, u32[]{:S(2)}) copy-start(bf16[2,512,512]{2,1,0:T(8,128)(2,1)} %get-tuple-element.105) | copy-start | bytes 3145732
  99.0 14.5 %copy-start.4 = (bf16[512,512]{1,0:T(8,128)(2,1)S(1)}, bf16[512,512]{1,0:T(8,128)(2,1)}, u32[]{:S(2)}) copy-start(bf16[512,512]{1,0:T(8,128)(2,1)} %get-tuple-element.103) | copy-start | bytes 1572868
  108.8 19.4 %collective-permute-start.3 = (bf16[512,640]{1,0:T(8,128)(2,1)S(1)}, bf16[512,640]{1,0:T(8,128)(2,1)S(1)}, u32[]{:S(2)}, u32[]{:S(2)}) collective-permute-start(bf16[512,640]{1,0:T(8,128)(2,1)S(1)} %get-tuple-element.69), channel_id=1, source_target_pairs={{0,16},{16,0},{1,17},{17,1},{2,18},{18,2},{3,19},{19,3},{4,20},{20... | collective-permute-start | bytes 1966088 | tf_op jit(solution)/shard_map/ppermute | solution.py:284
  109.4 31.1 %collective-permute-start.17 = (bf16[2,512,512]{2,1,0:T(8,128)(2,1)S(1)}, bf16[2,512,512]{2,1,0:T(8,128)(2,1)S(1)}, u32[]{:S(2)}, u32[]{:S(2)}) collective-permute-start(bf16[2,512,512]{2,1,0:T(8,128)(2,1)S(1)} %copy-done.2), channel_id=1, source_target_pairs={{0,15},{1,2},{2,1},{3,4},{4,3},{5,6},{6,5},{7,8},{8,7},{9,10},{10,... | collective-permute-start | bytes 3145736 | tf_op jit(solution)/shard_map/ppermute | solution.py:201
  113.4 27.1 %collective-permute-start.16 = (bf16[512,512]{1,0:T(8,128)(2,1)S(1)}, bf16[512,512]{1,0:T(8,128)(2,1)S(1)}, u32[]{:S(2)}, u32[]{:S(2)}) collective-permute-start(bf16[512,512]{1,0:T(8,128)(2,1)S(1)} %copy-done.4), channel_id=1, source_target_pairs={{0,16},{16,0},{1,17},{17,1},{2,18},{18,2},{3,19},{19,3},{4,20},{20... | collective-permute-start | bytes 1572872 | tf_op jit(solution)/shard_map/ppermute | solution.py:202
  125.7 23.7 %collective-permute-start.12 = (bf16[512,640]{1,0:T(8,128)(2,1)S(1)}, bf16[512,640]{1,0:T(8,128)(2,1)S(1)}, u32[]{:S(2)}, u32[]{:S(2)}) collective-permute-start(bf16[512,640]{1,0:T(8,128)(2,1)S(1)} %get-tuple-element.91), channel_id=1, source_target_pairs={{0,16},{16,0},{1,17},{17,1},{2,18},{18,2},{3,19},{19,3},{4,20},{20... | collective-permute-start | bytes 1966088 | tf_op jit(solution)/shard_map/ppermute | solution.py:284
  127.1 47.7 %collective-permute-start.14 = (bf16[2,512,256]{2,1,0:T(8,128)(2,1)S(1)}, bf16[2,512,256]{2,1,0:T(8,128)(2,1)S(1)}, u32[]{:S(2)}, u32[]{:S(2)}) collective-permute-start(bf16[2,512,256]{2,1,0:T(8,128)(2,1)S(1)} %slice.73), channel_id=1, source_target_pairs={{0,15},{1,2},{2,1},{3,4},{4,3},{5,6},{6,5},{7,8},{8,7},{9,10},{10,... | collective-permute-start | bytes 1572872 | tf_op jit(solution)/shard_map/ppermute | solution.py:201
  140.0 34.8 %collective-permute-start.9 = (bf16[512,640]{1,0:T(8,128)(2,1)S(1)}, bf16[512,640]{1,0:T(8,128)(2,1)S(1)}, u32[]{:S(2)}, u32[]{:S(2)}) collective-permute-start(bf16[512,640]{1,0:T(8,128)(2,1)S(1)} %get-tuple-element.83), channel_id=1, source_target_pairs={{0,16},{16,0},{1,17},{17,1},{2,18},{18,2},{3,19},{19,3},{4,20},{20... | collective-permute-start | bytes 1966088 | tf_op jit(solution)/shard_map/ppermute | solution.py:284
  161.3 25.3 %collective-permute-start.18 = (bf16[512,640]{1,0:T(8,128)(2,1)S(1)}, bf16[512,640]{1,0:T(8,128)(2,1)S(1)}, u32[]{:S(2)}, u32[]{:S(2)}) collective-permute-start(bf16[512,640]{1,0:T(8,128)(2,1)S(1)} %get-tuple-element.109), channel_id=1, source_target_pairs={{0,16},{16,0},{1,17},{17,1},{2,18},{18,2},{3,19},{19,3},{4,20},{20... | collective-permute-start | bytes 1966088 | tf_op jit(solution)/shard_map/ppermute | solution.py:284
  161.4 13.4 %collective-permute-start.13 = (bf16[512,256]{1,0:T(8,128)(2,1)S(1)}, bf16[512,256]{1,0:T(8,128)(2,1)S(1)}, u32[]{:S(2)}, u32[]{:S(2)}) collective-permute-start(bf16[512,256]{1,0:T(8,128)(2,1)S(1)} %slice.72), channel_id=1, source_target_pairs={{0,16},{16,0},{1,17},{17,1},{2,18},{18,2},{3,19},{19,3},{4,20},{20... | collective-permute-start | bytes 786440 | tf_op jit(solution)/shard_map/ppermute | solution.py:202
  182.8 12.8 %collective-permute-start.15 = (bf16[512,384]{1,0:T(8,128)(2,1)S(1)}, bf16[512,384]{1,0:T(8,128)(2,1)S(1)}, u32[]{:S(2)}, u32[]{:S(2)}) collective-permute-start(bf16[512,384]{1,0:T(8,128)(2,1)S(1)} %get-tuple-element.101), channel_id=1, source_target_pairs={{0,16},{16,0},{1,17},{17,1},{2,18},{18,2},{3,19},{19,3},{4,20},{20... | collective-permute-start | bytes 1179656 | tf_op jit(solution)/shard_map/ppermute | solution.py:284
  182.9 9.2 %collective-permute-start.23 = (bf16[2,512,128]{2,1,0:T(8,128)(2,1)S(1)}, bf16[2,512,128]{2,1,0:T(8,128)(2,1)S(1)}, u32[]{:S(2)}, u32[]{:S(2)}) collective-permute-start(bf16[2,512,128]{2,1,0:T(8,128)(2,1)S(1)} %get-tuple-element.120), channel_id=1, source_target_pairs={{0,15},{1,2},{2,1},{3,4},{4,3},{5,6},{6,5},{7,8},{8,7},{9,10},{10,... | collective-permute-start | bytes 786440 | tf_op jit(solution)/shard_map/ppermute | solution.py:201
  182.9 15.1 %collective-permute-start.20 = (bf16[2,512,128]{2,1,0:T(8,128)(2,1)S(1)}, bf16[2,512,128]{2,1,0:T(8,128)(2,1)S(1)}, u32[]{:S(2)}, u32[]{:S(2)}) collective-permute-start(bf16[2,512,128]{2,1,0:T(8,128)(2,1)S(1)} %get-tuple-element.114), channel_id=1, source_target_pairs={{0,15},{1,2},{2,1},{3,4},{4,3},{5,6},{6,5},{7,8},{8,7},{9,10},{10,... | collective-permute-start | bytes 786440 | tf_op jit(solution)/shard_map/ppermute | solution.py:201
  184.7 7.4 %collective-permute-start.22 = (bf16[512,128]{1,0:T(8,128)(2,1)S(1)}, bf16[512,128]{1,0:T(8,128)(2,1)S(1)}, u32[]{:S(2)}, u32[]{:S(2)}) collective-permute-start(bf16[512,128]{1,0:T(8,128)(2,1)S(1)} %get-tuple-element.119), channel_id=1, source_target_pairs={{0,16},{16,0},{1,17},{17,1},{2,18},{18,2},{3,19},{19,3},{4,20},{20... | collective-permute-start | bytes 393224 | tf_op jit(solution)/shard_map/ppermute | solution.py:202
  186.6 11.4 %collective-permute-start.19 = (bf16[512,128]{1,0:T(8,128)(2,1)S(1)}, bf16[512,128]{1,0:T(8,128)(2,1)S(1)}, u32[]{:S(2)}, u32[]{:S(2)}) collective-permute-start(bf16[512,128]{1,0:T(8,128)(2,1)S(1)} %get-tuple-element.113), channel_id=1, source_target_pairs={{0,16},{16,0},{1,17},{17,1},{2,18},{18,2},{3,19},{19,3},{4,20},{20... | collective-permute-start | bytes 393224 | tf_op jit(solution)/shard_map/ppermute | solution.py:202
  186.7 11.3 %slice-start = ((s8[6291456]{0:T(1024)(128)(4,1)}), s8[4194304]{0:T(1024)(128)(4,1)S(1)}, s32[]{:S(2)}) async-start(s8[6291456]{0:T(1024)(128)(4,1)} %bitcast.24), calls=%async_computation | async-start | bytes 8388608
  192.0 6.0 %slice-start.1 = ((s8[6291456]{0:T(1024)(128)(4,1)}), s8[2097152]{0:T(1024)(128)(4,1)S(1)}, s32[]{:S(2)}) async-start(s8[6291456]{0:T(1024)(128)(4,1)} %bitcast.24), calls=%async_computation.1 | async-start | bytes 4194304
  195.5 7.8 %collective-permute-start.24 = (bf16[512,256]{1,0:T(8,128)(2,1)S(1)}, bf16[512,256]{1,0:T(8,128)(2,1)S(1)}, u32[]{:S(2)}, u32[]{:S(2)}) collective-permute-start(bf16[512,256]{1,0:T(8,128)(2,1)S(1)} %get-tuple-element.123), channel_id=1, source_target_pairs={{0,16},{16,0},{1,17},{17,1},{2,18},{18,2},{3,19},{19,3},{4,20},{20... | collective-permute-start | bytes 786440 | tf_op jit(solution)/shard_map/ppermute | solution.py:284
  201.5 6.4 %collective-permute-start.21 = (bf16[512,256]{1,0:T(8,128)(2,1)S(1)}, bf16[512,256]{1,0:T(8,128)(2,1)S(1)}, u32[]{:S(2)}, u32[]{:S(2)}) collective-permute-start(bf16[512,256]{1,0:T(8,128)(2,1)S(1)} %get-tuple-element.117), channel_id=1, source_target_pairs={{0,16},{16,0},{1,17},{17,1},{2,18},{18,2},{3,19},{19,3},{4,20},{20... | collective-permute-start | bytes 786440 | tf_op jit(solution)/shard_map/ppermute | solution.py:284

commit v3 on v2

--- a/solution.py
+++ b/solution.py
@@ -15,15 +15,20 @@
 LOWEST = -3e38
 SPAN = 4
 LANES = 16
-SIZES = (4, 4, 4, 4, 4, 2, 1, 1)
+SIZES = (4, 4, 8, 8)
+ASKS = (4, 4, 16)
+MERGES = {2: 1, 3: 1}
 DEPTH = 2
-LAG = 2
 
 
 def group_sizes(heads):
     if sum(SIZES) == heads:
         return SIZES
     return (4,) * (heads // 4) + (1,) * (heads % 4)
+
+
+def ask_sizes(heads):
+    return ASKS if sum(ASKS) == heads else (heads,)
 
 
 def parts_of(x):
@@ -48,7 +53,7 @@
 
     def copies(which):
         for region, ref in enumerate((own_ref, even_ref, odd_ref)):
-            first = (which if region == 2 else start + which) * HEAD
+            first = (start + which if region == 1 else which) * HEAD
             yield pltpu.make_async_copy(
                 ref.at[:, :, :, pl.ds(pl.multiple_of(first, HEAD), HEAD)],
                 windows.at[which % 2, :, region * tiles : (region + 1) * tiles],
@@ -163,10 +168,6 @@
             out_ref[:, columns] = result.astype(out_ref.dtype)
 
 
-def after(value, *done):
-    return lax.optimization_barrier((value, *done))[0]
-
-
 def local(queries, key_values, neighbours, clean_section):
     tok_dev, feat = queries.shape[1:]
     tiles = tok_dev // TILE
@@ -190,23 +191,39 @@
 
     sizes = group_sizes(heads)
     starts = [sum(sizes[:g]) for g in range(len(sizes))]
-    odd, partner = [], []
-    even = None
-    for g, (start, size) in enumerate(zip(starts, sizes)):
-        low, high = start * HEAD, (start + size) * HEAD
-        block, ask = own[:, :, low:high], query[:, low:high]
+    groups = range(len(sizes))
+    cuts = [own[:, :, starts[g] * HEAD : (starts[g] + sizes[g]) * HEAD] for g in groups]
+    blocks, odd = [], []
+
+    def send(block):
+        blocks.append(block)
+        odd.append(lax.ppermute(block, "tile", odd_pairs))
+
+    for g in range(DEPTH):
+        send(cuts[g])
+    even = lax.ppermute(own, "tile", even_pairs)
+
+    partner = []
+    first = 0
+    for g, size in enumerate(ask_sizes(heads)):
+        ask = query[:, first * HEAD : (first + size) * HEAD]
         if g >= DEPTH:
-            block, odd[g - DEPTH] = lax.optimization_barrier((block, odd[g - DEPTH]))
-            ask, partner[g - DEPTH] = lax.optimization_barrier((ask, partner[g - DEPTH]))
-        odd.append(lax.ppermute(block, "tile", odd_pairs))
-        partner.append(lax.ppermute(ask, "section", swap))
-        if even is None:
-            even = lax.ppermute(own, "tile", even_pairs)
+            *held, moved = partner[g - DEPTH]
+            ask, moved = lax.optimization_barrier((ask, moved))
+            partner[g - DEPTH] = (*held, moved)
+        partner.append((first, size, lax.ppermute(ask, "section", swap)))
+        first += size
+
+    def partner_of(start):
+        for first, size, moved in partner:
+            if first <= start < first + size:
+                return start - first, moved
 
     def rows4(x):
         return x.reshape(2, tiles, TILE, x.shape[-1])
 
-    def attend(start, size, odd_part, partner_part, slots):
+    def attend(start, size, own_part, odd_part, slots):
+        skip, asked = partner_of(start)
         units = size * tiles * 2 * TILE * listed * TILE
         return pl.pallas_call(
             functools.partial(
@@ -217,7 +234,7 @@
                 grid=(size,),
                 in_specs=[
                     pl.BlockSpec((tok_dev, HEAD), lambda h, *_: (0, start + h)),
-                    pl.BlockSpec((tok_dev, HEAD), lambda h, *_: (0, h)),
+                    pl.BlockSpec((tok_dev, HEAD), lambda h, *_: (0, skip + h)),
                 ]
                 + [pl.BlockSpec(memory_space=pl.ANY)] * 3,
                 out_specs=[
@@ -244,7 +261,7 @@
                 dimension_semantics=("arbitrary",), vmem_limit_bytes=24 << 20
             ),
             name="attend",
-        )(slots, dead, query, partner_part, rows4(own), rows4(even), rows4(odd_part))
+        )(slots, dead, query, asked, rows4(own_part), rows4(even), rows4(odd_part))
 
     def merge(start, size, mine, stats, message, target):
         last = [] if target is None else [target]
@@ -268,7 +285,7 @@
                 bytes_accessed=size * HEAD * tok_dev * 2 * 3,
             ),
             compiler_params=pltpu.CompilerParams(
-                dimension_semantics=("arbitrary",), vmem_limit_bytes=16 << 20
+                dimension_semantics=("arbitrary",), vmem_limit_bytes=24 << 20
             ),
             name="merge",
         )(dead, mine, stats, message, *last)
@@ -277,11 +294,19 @@
     waiting = []
     for g, (start, size) in enumerate(zip(starts, sizes)):
         index = slots
-        if len(waiting) >= LAG:
+        if g:
+            index, stats = lax.optimization_barrier((index, waiting[-1][3]))
+            waiting[-1][3] = stats
+        for _ in range(MERGES.get(g, 0) if len(sizes) == len(SIZES) else 0):
             target = merge(*waiting.pop(0), target)
-            index, target = lax.optimization_barrier((slots, target))
-        mine, stats, message = attend(start, size, odd[g], partner[g], index)
-        waiting.append((start, size, mine, stats, lax.ppermute(message, "section", swap)))
+            index, target = lax.optimization_barrier((index, target))
+        if g + DEPTH < len(sizes):
+            block, odd[g] = lax.optimization_barrier((cuts[g + DEPTH], odd[g]))
+            if g:
+                block, waiting[-1][3] = lax.optimization_barrier((block, waiting[-1][3]))
+            send(block)
+        mine, stats, message = attend(start, size, blocks[g], odd[g], index)
+        waiting.append([start, size, mine, stats, lax.ppermute(message, "section", swap)])
     for item in waiting:
         target = merge(*item, target)
     return target[None]

time: 212 us -> 196 us (0.925)
  Pallas kernels: 79.6 us -> 62.3 us
  waiting for transfers between devices: 101 us -> 112 us
  starting transfers between devices: 20 us -> 12.4 us
    pallas_call x8 -> x4, Pallas kernels: 20.4 us -> 9.8 us  [merge(): pl.pallas_call(functools.partial(merge_kernel, heads=size), grid_spec=plt...]
    ppermute x16 -> x7, waiting for transfers between devices: 85.1 us -> 94.8 us  [the longest x4 73.3 us: send(): odd.append(lax.ppermute(block, 'tile', odd_pairs))]
    ppermute x16 -> x7, starting transfers between devices: 15.1 us -> 7.93 us  [the longest x3 4.47 us: local(): partner.append((first, size, lax.ppermute(ask, 'section', swap)))]
    pallas_call x8 -> x4, Pallas kernels: 59.2 us -> 52.5 us  [attend(): pl.pallas_call(functools.partial(attend_kernel, tiles=tiles, listed=liste...]
    unnamed x20 -> x10, local copies, waits for them, and re-layouts: 2.82 us -> 0.02 us
    slice x6 -> x4, local copies, waits for them, and re-layouts: 6.81 us -> 8.6 us  [the longest x2 6.05 us: local(): own[:, :, starts[g] * HEAD:(starts[g] + sizes[g]) * HEAD]]
    ppermute x8 -> x4, waiting for transfers between devices: 15.5 us -> 17 us  [local(): lax.ppermute(message, 'section', swap)]
    ppermute x8 -> x4, starting transfers between devices: 4.86 us -> 4.46 us  [local(): lax.ppermute(message, 'section', swap)]
  transfers between devices with their start and end apart: 25 -> 12, of which waited for: 7 -> 6; matrix products, arithmetic and copies ran while one was open for 3% -> 4% of each run, Pallas kernels for 37% -> 31%
where the time goes in v3:
time: 196 us; the launch traced here: 195 us
  waiting for transfers between devices  112 us (57%)
  Pallas kernels  62.3 us (32%)
  starting transfers between devices  12.4 us (6%)
  local copies, waits for them, and re-layouts  8.7 us (4%)
    ppermute x4, waiting for transfers between devices, send(): odd.append(lax.ppermute(block, 'tile', odd_pairs))  73.3 us
    pallas_call x4, Pallas kernels, attend(): pl.pallas_call(functools.partial(attend_kernel, tiles=tiles, listed=liste...  52.5 us
    ppermute x3, waiting for transfers between devices, local(): partner.append((first, size, lax.ppermute(ask, 'section', swap)))  21.5 us
    ppermute x4, waiting for transfers between devices, local(): lax.ppermute(message, 'section', swap)  17 us
    pallas_call x4, Pallas kernels, merge(): pl.pallas_call(functools.partial(merge_kernel, heads=size), grid_spec=plt...  9.8 us
    slice x2, local copies, waits for them, and re-layouts, local(): own[:, :, starts[g] * HEAD:(starts[g] + sizes[g]) * HEAD]  6.05 us
    ppermute x3, starting transfers between devices, local(): partner.append((first, size, lax.ppermute(ask, 'section', swap)))  4.47 us
    ppermute x4, starting transfers between devices, local(): lax.ppermute(message, 'section', swap)  4.46 us
  transfers between devices with their start and end apart: 12, of which 6 were waited for; matrix products, arithmetic and copies ran while one was open for 4% of the time, Pallas kernels for 31%

profile of v3, /device:TPU:12, one launch (start us, length us, event | category | flops | bytes accessed | tf_op | source)
XLA Modules:
  0.0 195.3 jit_solution(241674814063463925)
XLA Ops:
  0.0 0.0 copy-start
  0.0 0.0 collective-permute-start.1
  0.0 3.2 %fusion.3 = (bf16[2,512,512]{2,1,0:T(8,128)(2,1)}, bf16[2,512,512]{2,1,0:T(8,128)(2,1)}) fusion(bf16[2,512,3072]{2,1,0:T(8,128)(2,1)} %bitcast.23), kind=kLoop, calls=%fused_computation.10 | loop fusion | bytes 4194304 | tf_op jit(solution)/shard_map/slice | solution.py:195
  3.2 0.7 collective-permute-start.2
  4.0 1.0 collective-permute-start.4
  5.0 0.0 copy-done
  5.0 1.0 fusion.4
  6.0 1.5 collective-permute-start
  7.5 0.0 copy-start.3
  7.5 1.5 slice.28
  9.0 0.0 copy-done.3
  9.0 0.1 reshape.33.slots_ref
  9.1 0.0 copy-start.1
  9.1 0.0 copy-start.4
  9.1 2.8 %fusion.2 = (bf16[2,512,1024]{2,1,0:T(8,128)(2,1)S(1)}, bf16[2,512,1024]{2,1,0:T(8,128)(2,1)S(1)}) fusion(bf16[2,512,3072]{2,1,0:T(8,128)(2,1)} %bitcast.24), kind=kLoop, calls=%fused_computation.9 | loop fusion | bytes 8388608 | tf_op jit(solution)/shard_map/slice | solution.py:195
  12.0 8.7 %collective-permute-done.qp_ref = bf16[512,512]{1,0:T(8,128)(2,1)} collective-permute-done((bf16[512,512]{1,0:T(8,128)(2,1)}, bf16[512,512]{1,0:T(8,128)(2,1)}, u32[]{:S(2)}, u32[]{:S(2)}) %collective-permute-start) | collective-permute-done | bytes 524320 | tf_op jit(solution)/shard_map/ppermute | solution.py:214
  20.7 0.0 copy-done.1
  20.7 1.5 collective-permute-start.6
  22.2 63.0 %collective-permute-done.2 = bf16[2,512,512]{2,1,0:T(8,128)(2,1)} collective-permute-done((bf16[2,512,512]{2,1,0:T(8,128)(2,1)}, bf16[2,512,512]{2,1,0:T(8,128)(2,1)}, u32[]{:S(2)}, u32[]{:S(2)}) %collective-permute-start.2) | collective-permute-done | bytes 1048608 | tf_op jit(solution)/shard_map/ppermute | solution.py:200
  85.2 0.9 collective-permute-start.7
  86.1 0.0 copy-done.4
  86.1 10.3 %collective-permute-done.4 = bf16[2,512,512]{2,1,0:T(8,128)(2,1)} collective-permute-done((bf16[2,512,512]{2,1,0:T(8,128)(2,1)}, bf16[2,512,512]{2,1,0:T(8,128)(2,1)}, u32[]{:S(2)}, u32[]{:S(2)}) %collective-permute-start.4) | collective-permute-done | bytes 1048608 | tf_op jit(solution)/shard_map/ppermute | solution.py:200
  96.4 0.0 collective-permute-done.1
  96.4 0.0 copy-start.2
  96.4 9.7 %attend.4 = (bf16[512,512]{1,0:T(8,128)(2,1)S(1)}, f32[512,128]{1,0:T(8,128)S(1)}, bf16[512,640]{1,0:T(8,128)(2,1)S(1)}) custom-call(s32[32]{0:T(128)S(1)} %reshape.33.slots_ref, s32[4]{0:T(128)S(1)} %compare_convert_fusion.dead_ref, bf16[512,3072]{1,0:T(8,128)(2,1)S(1)} %bitcast.14, bf16[512,512]{1,0:T(8,128)(2,1)} %collective-permute-done.qp_ref, ...), custom_call_target="tpu_custom_call" | custom-call | flops 2147483648 | bytes 5242880 | tf_op jit(solution)/shard_map/attend/pallas_call | solution.py:228
  106.2 0.8 collective-permute-start.9
  107.0 0.0 copy-done.2
  107.0 1.5 collective-permute-start.3
  108.4 0.5 collective-permute-start.5
  109.0 12.8 %collective-permute-done.3.qp_ref = bf16[512,512]{1,0:T(8,128)(2,1)S(1)} collective-permute-done((bf16[512,512]{1,0:T(8,128)(2,1)S(1)}, bf16[512,512]{1,0:T(8,128)(2,1)S(1)}, u32[]{:S(2)}, u32[]{:S(2)}) %collective-permute-start.3) | collective-permute-done | bytes 524320 | tf_op jit(solution)/shard_map/ppermute | solution.py:214
  121.8 9.0 %attend.5 = (bf16[512,512]{1,0:T(8,128)(2,1)S(1)}, f32[512,128]{1,0:T(8,128)S(1)}, bf16[512,640]{1,0:T(8,128)(2,1)S(1)}) custom-call(s32[32]{0:T(128)S(1)} %reshape.33.slots_ref, s32[4]{0:T(128)S(1)} %compare_convert_fusion.dead_ref, bf16[512,3072]{1,0:T(8,128)(2,1)S(1)} %bitcast.15, bf16[512,512]{1,0:T(8,128)(2,1)S(1)} %collective-permute-done.3.qp_ref, ...), custom_call_target="tpu_custom_call" | custom-call | flops 2147483648 | bytes 5242880 | tf_op jit(solution)/shard_map/attend/pallas_call | solution.py:228
  130.7 1.6 collective-permute-start.8
  132.3 3.5 %collective-permute-done.5.msg_ref = bf16[512,640]{1,0:T(8,128)(2,1)S(1)} collective-permute-done((bf16[512,640]{1,0:T(8,128)(2,1)S(1)}, bf16[512,640]{1,0:T(8,128)(2,1)S(1)}, u32[]{:S(2)}, u32[]{:S(2)}) %collective-permute-start.5) | collective-permute-done | bytes 655392 | tf_op jit(solution)/shard_map/ppermute | solution.py:309
  135.8 2.3 %merge.4.rest_0_ = bf16[512,3072]{1,0:T(8,128)(2,1)} custom-call(s32[4]{0:T(128)S(1)} %compare_convert_fusion.dead_ref, bf16[512,512]{1,0:T(8,128)(2,1)S(1)} %get-tuple-element.42.own_ref, f32[512,128]{1,0:T(8,128)S(1)} %get-tuple-element.45.stat_ref, bf16[512,640]{1,0:T(8,128)(2,1)S(1)} %collective-permute-done.5.msg_ref), custom_call_target="tpu_custom_call" | custom-call | flops 2097152 | bytes 1572864 | tf_op jit(solution)/shard_map/merge/pallas_call | solution.py:268
  138.1 0.0 collective-permute-done.6.qp_ref
  138.1 0.0 collective-permute-done.7
  138.1 16.9 %attend.6 = (bf16[512,1024]{1,0:T(8,128)(2,1)S(1)}, f32[512,128]{1,0:T(8,128)S(1)}, bf16[512,1152]{1,0:T(8,128)(2,1)S(1)}) custom-call(s32[32]{0:T(128)S(1)} %reshape.33.slots_ref, s32[4]{0:T(128)S(1)} %compare_convert_fusion.dead_ref, bf16[512,3072]{1,0:T(8,128)(2,1)S(1)} %bitcast.16, bf16[512,2048]{1,0:T(8,128)(2,1)S(1)} %collective-permute-done.6.qp_ref, ...), custom_call_target="tpu_custom_call" | custom-call | flops 4294967296 | bytes 10485760 | tf_op jit(solution)/shard_map/attend/pallas_call | solution.py:228
  155.0 0.0 collective-permute-done.8.msg_ref
  155.0 2.3 %merge.5.rest_0_ = bf16[512,3072]{1,0:T(8,128)(2,1)} custom-call(s32[4]{0:T(128)S(1)} %compare_convert_fusion.dead_ref, bf16[512,512]{1,0:T(8,128)(2,1)S(1)} %get-tuple-element.52.own_ref, f32[512,128]{1,0:T(8,128)S(1)} %get-tuple-element.53.stat_ref, bf16[512,640]{1,0:T(8,128)(2,1)S(1)} %collective-permute-done.8.msg_ref, ...), custom_call_target="tpu_custom_call", output_to_operand_aliasing={{}: (4, {})} | custom-call | flops 2097152 | bytes 1572864 | tf_op jit(solution)/shard_map/merge/pallas_call | solution.py:268
  157.3 2.2 %collective-permute-start.11 = (bf16[512,1152]{1,0:T(8,128)(2,1)S(1)}, bf16[512,1152]{1,0:T(8,128)(2,1)S(1)}, u32[]{:S(2)}, u32[]{:S(2)}) collective-permute-start(bf16[512,1152]{1,0:T(8,128)(2,1)S(1)} %get-tuple-element.63), channel_id=1, source_target_pairs={{0,16},{16,0},{1,17},{17,1},{2,18},{18,2},{3,19},{19,3},{4,20},{20... | collective-permute-start | bytes 3538952 | tf_op jit(solution)/shard_map/ppermute | solution.py:309
  159.6 0.0 collective-permute-done.9
  159.6 16.9 %attend.7 = (bf16[512,1024]{1,0:T(8,128)(2,1)S(1)}, f32[512,128]{1,0:T(8,128)S(1)}, bf16[512,1152]{1,0:T(8,128)(2,1)S(1)}) custom-call(s32[32]{0:T(128)S(1)} %reshape.33.slots_ref, s32[4]{0:T(128)S(1)} %compare_convert_fusion.dead_ref, bf16[512,3072]{1,0:T(8,128)(2,1)S(1)} %bitcast.17, bf16[512,2048]{1,0:T(8,128)(2,1)S(1)} %collective-permute-done.6.qp_ref, ...), custom_call_target="tpu_custom_call" | custom-call | flops 4294967296 | bytes 10485760 | tf_op jit(solution)/shard_map/attend/pallas_call | solution.py:228
  176.5 0.1 collective-permute-start.10
  176.6 0.0 collective-permute-done.11.msg_ref
  176.6 2.6 %merge.6.rest_0_ = bf16[512,3072]{1,0:T(8,128)(2,1)} custom-call(s32[4]{0:T(128)S(1)} %compare_convert_fusion.dead_ref, bf16[512,1024]{1,0:T(8,128)(2,1)S(1)} %get-tuple-element.61.own_ref, f32[512,128]{1,0:T(8,128)S(1)} %get-tuple-element.62.stat_ref, bf16[512,1152]{1,0:T(8,128)(2,1)S(1)} %collective-permute-done.11.msg_ref, ...), custom_call_target="tpu_custom_call", output_to_operand_aliasing={{}: (4, {})} | custom-call | flops 4194304 | bytes 3145728 | tf_op jit(solution)/shard_map/merge/pallas_call | solution.py:268
  179.2 13.6 %collective-permute-done.10.msg_ref = bf16[512,1152]{1,0:T(8,128)(2,1)S(1)} collective-permute-done((bf16[512,1152]{1,0:T(8,128)(2,1)S(1)}, bf16[512,1152]{1,0:T(8,128)(2,1)S(1)}, u32[]{:S(2)}, u32[]{:S(2)}) %collective-permute-start.10) | collective-permute-done | bytes 1179680 | tf_op jit(solution)/shard_map/ppermute | solution.py:309
  192.8 2.6 %merge.7 = bf16[512,3072]{1,0:T(8,128)(2,1)} custom-call(s32[4]{0:T(128)S(1)} %compare_convert_fusion.dead_ref, bf16[512,1024]{1,0:T(8,128)(2,1)S(1)} %get-tuple-element.58.own_ref, f32[512,128]{1,0:T(8,128)S(1)} %get-tuple-element.59.stat_ref, bf16[512,1152]{1,0:T(8,128)(2,1)S(1)} %collective-permute-done.10.msg_ref, ...), custom_call_target="tpu_custom_call", output_to_operand_aliasing={{}: (4, {})} | custom-call | flops 4194304 | bytes 3145728 | tf_op jit(solution)/shard_map/merge/pallas_call | solution.py:268
  (2 shorter events, 0.0 us)
Async XLA Ops:
  0.0 5.0 %copy-start = (bf16[1,512,3072]{2,1,0:T(8,128)(2,1)S(1)}, bf16[1,512,3072]{2,1,0:T(8,128)(2,1)}, u32[]{:S(2)}) copy-start(bf16[1,512,3072]{2,1,0:T(8,128)(2,1)} %param.4) | copy-start | bytes 9437188
  0.0 96.4 %collective-permute-start.1 = (bf16[2,512,3072]{2,1,0:T(8,128)(2,1)}, bf16[2,512,3072]{2,1,0:T(8,128)(2,1)}, u32[]{:S(2)}, u32[]{:S(2)}) collective-permute-start(bf16[2,512,3072]{2,1,0:T(8,128)(2,1)} %bitcast.22), channel_id=1, source_target_pairs={{0,1},{1,0},{2,3},{3,2},{4,5},{5,4},{6,7},{7,6},{8,9},{9,8},{10,11... | collective-permute-start | bytes 18874376 | tf_op jit(solution)/shard_map/ppermute | solution.py:204
  3.2 82.0 %collective-permute-start.2 = (bf16[2,512,512]{2,1,0:T(8,128)(2,1)}, bf16[2,512,512]{2,1,0:T(8,128)(2,1)}, u32[]{:S(2)}, u32[]{:S(2)}) collective-permute-start(bf16[2,512,512]{2,1,0:T(8,128)(2,1)} %get-tuple-element.68), channel_id=1, source_target_pairs={{0,15},{1,2},{2,1},{3,4},{4,3},{5,6},{6,5},{7,8},{8,7},{9,10},{10,... | collective-permute-start | bytes 3145736 | tf_op jit(solution)/shard_map/ppermute | solution.py:200
  4.0 92.5 %collective-permute-start.4 = (bf16[2,512,512]{2,1,0:T(8,128)(2,1)}, bf16[2,512,512]{2,1,0:T(8,128)(2,1)}, u32[]{:S(2)}, u32[]{:S(2)}) collective-permute-start(bf16[2,512,512]{2,1,0:T(8,128)(2,1)} %get-tuple-element.67), channel_id=1, source_target_pairs={{0,15},{1,2},{2,1},{3,4},{4,3},{5,6},{6,5},{7,8},{8,7},{9,10},{10,... | collective-permute-start | bytes 3145736 | tf_op jit(solution)/shard_map/ppermute | solution.py:200
  6.0 14.6 %collective-permute-start = (bf16[512,512]{1,0:T(8,128)(2,1)}, bf16[512,512]{1,0:T(8,128)(2,1)}, u32[]{:S(2)}, u32[]{:S(2)}) collective-permute-start(bf16[512,512]{1,0:T(8,128)(2,1)} %get-tuple-element.70), channel_id=1, source_target_pairs={{0,16},{16,0},{1,17},{17,1},{2,18},{18,2},{3,19},{19,3},{4,20},{20... | collective-permute-start | bytes 1572872 | tf_op jit(solution)/shard_map/ppermute | solution.py:214
  7.5 1.5 copy-start.3
  9.1 11.5 %copy-start.1 = (bf16[512,2048]{1,0:T(8,128)(2,1)S(1)}, bf16[512,2048]{1,0:T(8,128)(2,1)}, u32[]{:S(2)}) copy-start(bf16[512,2048]{1,0:T(8,128)(2,1)} %slice.28) | copy-start | bytes 6291460
  9.1 77.0 %copy-start.4 = (s32[4]{0:T(128)S(1)}, s32[4]{0:T(128)}, u32[]{:S(2)}) copy-start(s32[4]{0:T(128)} %param.7) | copy-start | bytes 52
  20.7 117.4 %collective-permute-start.6 = (bf16[512,2048]{1,0:T(8,128)(2,1)S(1)}, bf16[512,2048]{1,0:T(8,128)(2,1)S(1)}, u32[]{:S(2)}, u32[]{:S(2)}) collective-permute-start(bf16[512,2048]{1,0:T(8,128)(2,1)S(1)} %copy-done.1), channel_id=1, source_target_pairs={{0,16},{16,0},{1,17},{17,1},{2,18},{18,2},{3,19},{19,3},{4,20},{20... | collective-permute-start | bytes 6291464 | tf_op jit(solution)/shard_map/ppermute | solution.py:214
  85.2 52.9 %collective-permute-start.7 = (bf16[2,512,1024]{2,1,0:T(8,128)(2,1)S(1)}, bf16[2,512,1024]{2,1,0:T(8,128)(2,1)S(1)}, u32[]{:S(2)}, u32[]{:S(2)}) collective-permute-start(bf16[2,512,1024]{2,1,0:T(8,128)(2,1)S(1)} %get-tuple-element.49), channel_id=1, source_target_pairs={{0,15},{1,2},{2,1},{3,4},{4,3},{5,6},{6,5},{7,8},{8,7},{9,10},{10,... | collective-permute-start | bytes 6291464 | tf_op jit(solution)/shard_map/ppermute | solution.py:200
  96.4 10.5 %copy-start.2 = (bf16[512,512]{1,0:T(8,128)(2,1)S(1)}, bf16[512,512]{1,0:T(8,128)(2,1)}, u32[]{:S(2)}) copy-start(bf16[512,512]{1,0:T(8,128)(2,1)} %get-tuple-element.69) | copy-start | bytes 1572868
  106.2 53.4 %collective-permute-start.9 = (bf16[2,512,1024]{2,1,0:T(8,128)(2,1)S(1)}, bf16[2,512,1024]{2,1,0:T(8,128)(2,1)S(1)}, u32[]{:S(2)}, u32[]{:S(2)}) collective-permute-start(bf16[2,512,1024]{2,1,0:T(8,128)(2,1)S(1)} %get-tuple-element.57), channel_id=1, source_target_pairs={{0,15},{1,2},{2,1},{3,4},{4,3},{5,6},{6,5},{7,8},{8,7},{9,10},{10,... | collective-permute-start | bytes 6291464 | tf_op jit(solution)/shard_map/ppermute | solution.py:200
  107.0 14.8 %collective-permute-start.3 = (bf16[512,512]{1,0:T(8,128)(2,1)S(1)}, bf16[512,512]{1,0:T(8,128)(2,1)S(1)}, u32[]{:S(2)}, u32[]{:S(2)}) collective-permute-start(bf16[512,512]{1,0:T(8,128)(2,1)S(1)} %copy-done.2), channel_id=1, source_target_pairs={{0,16},{16,0},{1,17},{17,1},{2,18},{18,2},{3,19},{19,3},{4,20},{20... | collective-permute-start | bytes 1572872 | tf_op jit(solution)/shard_map/ppermute | solution.py:214
  108.4 27.3 %collective-permute-start.5 = (bf16[512,640]{1,0:T(8,128)(2,1)S(1)}, bf16[512,640]{1,0:T(8,128)(2,1)S(1)}, u32[]{:S(2)}, u32[]{:S(2)}) collective-permute-start(bf16[512,640]{1,0:T(8,128)(2,1)S(1)} %get-tuple-element.46), channel_id=1, source_target_pairs={{0,16},{16,0},{1,17},{17,1},{2,18},{18,2},{3,19},{19,3},{4,20},{20... | collective-permute-start | bytes 1966088 | tf_op jit(solution)/shard_map/ppermute | solution.py:309
  130.7 24.3 %collective-permute-start.8 = (bf16[512,640]{1,0:T(8,128)(2,1)S(1)}, bf16[512,640]{1,0:T(8,128)(2,1)S(1)}, u32[]{:S(2)}, u32[]{:S(2)}) collective-permute-start(bf16[512,640]{1,0:T(8,128)(2,1)S(1)} %get-tuple-element.54), channel_id=1, source_target_pairs={{0,16},{16,0},{1,17},{17,1},{2,18},{18,2},{3,19},{19,3},{4,20},{20... | collective-permute-start | bytes 1966088 | tf_op jit(solution)/shard_map/ppermute | solution.py:309
  157.3 19.2 %collective-permute-start.11 = (bf16[512,1152]{1,0:T(8,128)(2,1)S(1)}, bf16[512,1152]{1,0:T(8,128)(2,1)S(1)}, u32[]{:S(2)}, u32[]{:S(2)}) collective-permute-start(bf16[512,1152]{1,0:T(8,128)(2,1)S(1)} %get-tuple-element.63), channel_id=1, source_target_pairs={{0,16},{16,0},{1,17},{17,1},{2,18},{18,2},{3,19},{19,3},{4,20},{20... | collective-permute-start | bytes 3538952 | tf_op jit(solution)/shard_map/ppermute | solution.py:309
  176.5 16.3 %collective-permute-start.10 = (bf16[512,1152]{1,0:T(8,128)(2,1)S(1)}, bf16[512,1152]{1,0:T(8,128)(2,1)S(1)}, u32[]{:S(2)}, u32[]{:S(2)}) collective-permute-start(bf16[512,1152]{1,0:T(8,128)(2,1)S(1)} %get-tuple-element.60), channel_id=1, source_target_pairs={{0,16},{16,0},{1,17},{17,1},{2,18},{18,2},{3,19},{19,3},{4,20},{20... | collective-permute-start | bytes 3538952 | tf_op jit(solution)/shard_map/ppermute | solution.py:309

commit v4 on v3

--- a/solution.py
+++ b/solution.py
@@ -292,6 +292,7 @@
 
     target = None
     waiting = []
+    pace = jnp.zeros((8, HEAD), jnp.float32)
     for g, (start, size) in enumerate(zip(starts, sizes)):
         index = slots
         if g:
@@ -301,9 +302,13 @@
             target = merge(*waiting.pop(0), target)
             index, target = lax.optimization_barrier((index, target))
         if g + DEPTH < len(sizes):
-            block, odd[g] = lax.optimization_barrier((cuts[g + DEPTH], odd[g]))
+            pace, odd[g] = lax.optimization_barrier((pace, odd[g]))
+            pace = lax.ppermute(pace, "tile", even_pairs)
+            block = cuts[g + DEPTH]
             if g:
-                block, waiting[-1][3] = lax.optimization_barrier((block, waiting[-1][3]))
+                block, pace, waiting[-1][3] = lax.optimization_barrier((block, pace, waiting[-1][3]))
+            else:
+                block, pace = lax.optimization_barrier((block, pace))
             send(block)
         mine, stats, message = attend(start, size, blocks[g], odd[g], index)
         waiting.append([start, size, mine, stats, lax.ppermute(message, "section", swap)])

time: 196 us -> 179 us (0.913)
  waiting for transfers between devices: 112 us -> 90.4 us
    ppermute x3, waiting for transfers between devices: 21.5 us -> 12.7 us  [local(): partner.append((first, size, lax.ppermute(ask, 'section', swap)))]
    ppermute x4, waiting for transfers between devices: 73.3 us -> 65.5 us  [send(): odd.append(lax.ppermute(block, 'tile', odd_pairs))]
    ppermute x4, waiting for transfers between devices: 17 us -> 12.2 us  [local(): lax.ppermute(message, 'section', swap)]
  transfers between devices with their start and end apart: 12 -> 12, of which waited for: 6 -> 7; matrix products, arithmetic and copies ran while one was open for 4% -> 6% of each run, Pallas kernels for 31% -> 33%
where the time goes in v4:
time: 179 us; the launch traced here: 177 us
  waiting for transfers between devices  90.4 us (51%)
  Pallas kernels  61.8 us (35%)
  starting transfers between devices  14.1 us (8%)
  local copies, waits for them, and re-layouts  10.5 us (6%)
    ppermute x4, waiting for transfers between devices, send(): odd.append(lax.ppermute(block, 'tile', odd_pairs))  65.5 us
    pallas_call x4, Pallas kernels, attend(): pl.pallas_call(functools.partial(attend_kernel, tiles=tiles, listed=liste...  52 us
    ppermute x3, waiting for transfers between devices, local(): partner.append((first, size, lax.ppermute(ask, 'section', swap)))  12.7 us
    ppermute x4, waiting for transfers between devices, local(): lax.ppermute(message, 'section', swap)  12.2 us
    pallas_call x4, Pallas kernels, merge(): pl.pallas_call(functools.partial(merge_kernel, heads=size), grid_spec=plt...  9.79 us
    slice x2, local copies, waits for them, and re-layouts, local(): own[:, :, starts[g] * HEAD:(starts[g] + sizes[g]) * HEAD]  7.84 us
    ppermute x4, starting transfers between devices, local(): lax.ppermute(message, 'section', swap)  6.21 us
    ppermute x3, starting transfers between devices, local(): partner.append((first, size, lax.ppermute(ask, 'section', swap)))  4.47 us
  transfers between devices with their start and end apart: 12, of which 7 were waited for; matrix products, arithmetic and copies ran while one was open for 6% of the time, Pallas kernels for 33%

profile of v4, /device:TPU:12, one launch (start us, length us, event | category | flops | bytes accessed | tf_op | source)
XLA Modules:
  0.0 177.0 jit_solution(15951138889592811149)
XLA Ops:
  0.0 0.0 copy-start
  0.0 0.0 collective-permute-start.1
  0.0 3.2 %fusion.3 = (bf16[2,512,512]{2,1,0:T(8,128)(2,1)}, bf16[2,512,512]{2,1,0:T(8,128)(2,1)}) fusion(bf16[2,512,3072]{2,1,0:T(8,128)(2,1)} %bitcast.21), kind=kLoop, calls=%fused_computation.10 | loop fusion | bytes 4194304 | tf_op jit(solution)/shard_map/slice | solution.py:195
  3.2 0.7 collective-permute-start.2
  3.9 0.0 copy-done
  3.9 1.1 fusion.4
  5.0 1.5 collective-permute-start
  6.4 0.7 collective-permute-start.4
  7.2 4.7 %fusion.2 = (bf16[2,512,1024]{2,1,0:T(8,128)(2,1)}, bf16[2,512,1024]{2,1,0:T(8,128)(2,1)}) fusion(bf16[2,512,3072]{2,1,0:T(8,128)(2,1)} %bitcast.22), kind=kLoop, calls=%fused_computation.9 | loop fusion | bytes 8388608 | tf_op jit(solution)/shard_map/slice | solution.py:195
  11.9 1.0 collective-permute-start.7
  12.9 0.0 copy-start.3
  12.9 0.0 copy-start.4
  12.9 1.5 slice.28
  14.4 0.0 copy-done.3
  14.4 0.1 reshape.33.slots_ref
  14.5 5.5 %collective-permute-done.qp_ref = bf16[512,512]{1,0:T(8,128)(2,1)} collective-permute-done((bf16[512,512]{1,0:T(8,128)(2,1)}, bf16[512,512]{1,0:T(8,128)(2,1)}, u32[]{:S(2)}, u32[]{:S(2)}) %collective-permute-start) | collective-permute-done | bytes 524320 | tf_op jit(solution)/shard_map/ppermute | solution.py:214
  20.0 1.5 collective-permute-start.6
  21.5 0.0 copy-done.4
  21.5 63.6 %collective-permute-done.2 = bf16[2,512,512]{2,1,0:T(8,128)(2,1)} collective-permute-done((bf16[2,512,512]{2,1,0:T(8,128)(2,1)}, bf16[2,512,512]{2,1,0:T(8,128)(2,1)}, u32[]{:S(2)}, u32[]{:S(2)}) %collective-permute-start.2) | collective-permute-done | bytes 1048608 | tf_op jit(solution)/shard_map/ppermute | solution.py:200
  85.1 0.0 collective-permute-done.1
  85.1 0.0 copy-start.1
  85.1 0.0 copy-start.2
  85.1 9.9 %attend.4 = (bf16[512,512]{1,0:T(8,128)(2,1)S(1)}, f32[512,128]{1,0:T(8,128)S(1)}, bf16[512,640]{1,0:T(8,128)(2,1)S(1)}) custom-call(s32[32]{0:T(128)S(1)} %reshape.33.slots_ref, s32[4]{0:T(128)S(1)} %compare_convert_fusion.dead_ref, bf16[512,3072]{1,0:T(8,128)(2,1)S(1)} %bitcast.14, bf16[512,512]{1,0:T(8,128)(2,1)} %collective-permute-done.qp_ref, ...), custom_call_target="tpu_custom_call" | custom-call | flops 2147483648 | bytes 5242880 | tf_op jit(solution)/shard_map/attend/pallas_call | solution.py:228
  95.1 0.0 copy-done.1
  95.1 1.0 collective-permute-start.9
  96.0 0.0 copy-done.2
  96.0 1.5 collective-permute-start.3
  97.5 0.0 collective-permute-done.4
  97.5 0.5 collective-permute-start.5
  98.1 7.2 %collective-permute-done.3.qp_ref = bf16[512,512]{1,0:T(8,128)(2,1)S(1)} collective-permute-done((bf16[512,512]{1,0:T(8,128)(2,1)S(1)}, bf16[512,512]{1,0:T(8,128)(2,1)S(1)}, u32[]{:S(2)}, u32[]{:S(2)}) %collective-permute-start.3) | collective-permute-done | bytes 524320 | tf_op jit(solution)/shard_map/ppermute | solution.py:214
  105.2 9.0 %attend.5 = (bf16[512,512]{1,0:T(8,128)(2,1)S(1)}, f32[512,128]{1,0:T(8,128)S(1)}, bf16[512,640]{1,0:T(8,128)(2,1)S(1)}) custom-call(s32[32]{0:T(128)S(1)} %reshape.33.slots_ref, s32[4]{0:T(128)S(1)} %compare_convert_fusion.dead_ref, bf16[512,3072]{1,0:T(8,128)(2,1)S(1)} %bitcast.15, bf16[512,512]{1,0:T(8,128)(2,1)S(1)} %collective-permute-done.3.qp_ref, ...), custom_call_target="tpu_custom_call" | custom-call | flops 2147483648 | bytes 5242880 | tf_op jit(solution)/shard_map/attend/pallas_call | solution.py:228
  114.2 1.6 collective-permute-start.8
  115.8 0.1 collective-permute-done.5.msg_ref
  115.9 2.3 %merge.4.rest_0_ = bf16[512,3072]{1,0:T(8,128)(2,1)} custom-call(s32[4]{0:T(128)S(1)} %compare_convert_fusion.dead_ref, bf16[512,512]{1,0:T(8,128)(2,1)S(1)} %get-tuple-element.36.own_ref, f32[512,128]{1,0:T(8,128)S(1)} %get-tuple-element.38.stat_ref, bf16[512,640]{1,0:T(8,128)(2,1)S(1)} %collective-permute-done.5.msg_ref), custom_call_target="tpu_custom_call" | custom-call | flops 2097152 | bytes 1572864 | tf_op jit(solution)/shard_map/merge/pallas_call | solution.py:268
  118.2 0.6 collective-permute-done.7
  118.8 0.0 collective-permute-done.6.qp_ref
  118.8 16.2 %attend.6 = (bf16[512,1024]{1,0:T(8,128)(2,1)S(1)}, f32[512,128]{1,0:T(8,128)S(1)}, bf16[512,1152]{1,0:T(8,128)(2,1)S(1)}) custom-call(s32[32]{0:T(128)S(1)} %reshape.33.slots_ref, s32[4]{0:T(128)S(1)} %compare_convert_fusion.dead_ref, bf16[512,3072]{1,0:T(8,128)(2,1)S(1)} %bitcast.16, bf16[512,2048]{1,0:T(8,128)(2,1)S(1)} %collective-permute-done.6.qp_ref, ...), custom_call_target="tpu_custom_call" | custom-call | flops 4294967296 | bytes 10485760 | tf_op jit(solution)/shard_map/attend/pallas_call | solution.py:228
  135.1 0.0 collective-permute-done.8.msg_ref
  135.1 2.3 %merge.5.rest_0_ = bf16[512,3072]{1,0:T(8,128)(2,1)} custom-call(s32[4]{0:T(128)S(1)} %compare_convert_fusion.dead_ref, bf16[512,512]{1,0:T(8,128)(2,1)S(1)} %get-tuple-element.44.own_ref, f32[512,128]{1,0:T(8,128)S(1)} %get-tuple-element.45.stat_ref, bf16[512,640]{1,0:T(8,128)(2,1)S(1)} %collective-permute-done.8.msg_ref, ...), custom_call_target="tpu_custom_call", output_to_operand_aliasing={{}: (4, {})} | custom-call | flops 2097152 | bytes 1572864 | tf_op jit(solution)/shard_map/merge/pallas_call | solution.py:268
  137.4 2.6 %collective-permute-start.11 = (bf16[512,1152]{1,0:T(8,128)(2,1)S(1)}, bf16[512,1152]{1,0:T(8,128)(2,1)S(1)}, u32[]{:S(2)}, u32[]{:S(2)}) collective-permute-start(bf16[512,1152]{1,0:T(8,128)(2,1)S(1)} %get-tuple-element.55), channel_id=1, source_target_pairs={{0,16},{16,0},{1,17},{17,1},{2,18},{18,2},{3,19},{19,3},{4,20},{20... | collective-permute-start | bytes 3538952 | tf_op jit(solution)/shard_map/ppermute | solution.py:314
  139.9 1.3 collective-permute-done.9
  141.2 16.9 %attend.7 = (bf16[512,1024]{1,0:T(8,128)(2,1)S(1)}, f32[512,128]{1,0:T(8,128)S(1)}, bf16[512,1152]{1,0:T(8,128)(2,1)S(1)}) custom-call(s32[32]{0:T(128)S(1)} %reshape.33.slots_ref, s32[4]{0:T(128)S(1)} %compare_convert_fusion.dead_ref, bf16[512,3072]{1,0:T(8,128)(2,1)S(1)} %bitcast.17, bf16[512,2048]{1,0:T(8,128)(2,1)S(1)} %collective-permute-done.6.qp_ref, ...), custom_call_target="tpu_custom_call" | custom-call | flops 4294967296 | bytes 10485760 | tf_op jit(solution)/shard_map/attend/pallas_call | solution.py:228
  158.1 1.6 collective-permute-start.10
  159.7 0.0 collective-permute-done.11.msg_ref
  159.7 2.6 %merge.6.rest_0_ = bf16[512,3072]{1,0:T(8,128)(2,1)} custom-call(s32[4]{0:T(128)S(1)} %compare_convert_fusion.dead_ref, bf16[512,1024]{1,0:T(8,128)(2,1)S(1)} %get-tuple-element.53.own_ref, f32[512,128]{1,0:T(8,128)S(1)} %get-tuple-element.54.stat_ref, bf16[512,1152]{1,0:T(8,128)(2,1)S(1)} %collective-permute-done.11.msg_ref, ...), custom_call_target="tpu_custom_call", output_to_operand_aliasing={{}: (4, {})} | custom-call | flops 4194304 | bytes 3145728 | tf_op jit(solution)/shard_map/merge/pallas_call | solution.py:268
  162.3 12.1 %collective-permute-done.10.msg_ref = bf16[512,1152]{1,0:T(8,128)(2,1)S(1)} collective-permute-done((bf16[512,1152]{1,0:T(8,128)(2,1)S(1)}, bf16[512,1152]{1,0:T(8,128)(2,1)S(1)}, u32[]{:S(2)}, u32[]{:S(2)}) %collective-permute-start.10) | collective-permute-done | bytes 1179680 | tf_op jit(solution)/shard_map/ppermute | solution.py:314
  174.4 2.6 %merge.7 = bf16[512,3072]{1,0:T(8,128)(2,1)} custom-call(s32[4]{0:T(128)S(1)} %compare_convert_fusion.dead_ref, bf16[512,1024]{1,0:T(8,128)(2,1)S(1)} %get-tuple-element.50.own_ref, f32[512,128]{1,0:T(8,128)S(1)} %get-tuple-element.51.stat_ref, bf16[512,1152]{1,0:T(8,128)(2,1)S(1)} %collective-permute-done.10.msg_ref, ...), custom_call_target="tpu_custom_call", output_to_operand_aliasing={{}: (4, {})} | custom-call | flops 4194304 | bytes 3145728 | tf_op jit(solution)/shard_map/merge/pallas_call | solution.py:268
  (2 shorter events, 0.0 us)
Async XLA Ops:
  0.0 3.9 %copy-start = (bf16[1,512,3072]{2,1,0:T(8,128)(2,1)S(1)}, bf16[1,512,3072]{2,1,0:T(8,128)(2,1)}, u32[]{:S(2)}) copy-start(bf16[1,512,3072]{2,1,0:T(8,128)(2,1)} %param.4) | copy-start | bytes 9437188
  0.0 85.1 %collective-permute-start.1 = (bf16[2,512,3072]{2,1,0:T(8,128)(2,1)}, bf16[2,512,3072]{2,1,0:T(8,128)(2,1)}, u32[]{:S(2)}, u32[]{:S(2)}) collective-permute-start(bf16[2,512,3072]{2,1,0:T(8,128)(2,1)} %bitcast.20), channel_id=1, source_target_pairs={{0,1},{1,0},{2,3},{3,2},{4,5},{5,4},{6,7},{7,6},{8,9},{9,8},{10,11... | collective-permute-start | bytes 18874376 | tf_op jit(solution)/shard_map/ppermute | solution.py:204
  3.2 82.0 %collective-permute-start.2 = (bf16[2,512,512]{2,1,0:T(8,128)(2,1)}, bf16[2,512,512]{2,1,0:T(8,128)(2,1)}, u32[]{:S(2)}, u32[]{:S(2)}) collective-permute-start(bf16[2,512,512]{2,1,0:T(8,128)(2,1)} %get-tuple-element.60), channel_id=1, source_target_pairs={{0,15},{1,2},{2,1},{3,4},{4,3},{5,6},{6,5},{7,8},{8,7},{9,10},{10,... | collective-permute-start | bytes 3145736 | tf_op jit(solution)/shard_map/ppermute | solution.py:200
  5.0 15.1 %collective-permute-start = (bf16[512,512]{1,0:T(8,128)(2,1)}, bf16[512,512]{1,0:T(8,128)(2,1)}, u32[]{:S(2)}, u32[]{:S(2)}) collective-permute-start(bf16[512,512]{1,0:T(8,128)(2,1)} %get-tuple-element.62), channel_id=1, source_target_pairs={{0,16},{16,0},{1,17},{17,1},{2,18},{18,2},{3,19},{19,3},{4,20},{20... | collective-permute-start | bytes 1572872 | tf_op jit(solution)/shard_map/ppermute | solution.py:214
  6.4 91.1 %collective-permute-start.4 = (bf16[2,512,512]{2,1,0:T(8,128)(2,1)}, bf16[2,512,512]{2,1,0:T(8,128)(2,1)}, u32[]{:S(2)}, u32[]{:S(2)}) collective-permute-start(bf16[2,512,512]{2,1,0:T(8,128)(2,1)} %get-tuple-element.59), channel_id=1, source_target_pairs={{0,15},{1,2},{2,1},{3,4},{4,3},{5,6},{6,5},{7,8},{8,7},{9,10},{10,... | collective-permute-start | bytes 3145736 | tf_op jit(solution)/shard_map/ppermute | solution.py:200
  11.9 107.0 %collective-permute-start.7 = (bf16[2,512,1024]{2,1,0:T(8,128)(2,1)}, bf16[2,512,1024]{2,1,0:T(8,128)(2,1)}, u32[]{:S(2)}, u32[]{:S(2)}) collective-permute-start(bf16[2,512,1024]{2,1,0:T(8,128)(2,1)} %get-tuple-element.57), channel_id=1, source_target_pairs={{0,15},{1,2},{2,1},{3,4},{4,3},{5,6},{6,5},{7,8},{8,7},{9,10},{10,... | collective-permute-start | bytes 6291464 | tf_op jit(solution)/shard_map/ppermute | solution.py:200
  12.9 1.5 copy-start.3
  12.9 8.6 %copy-start.4 = (s32[4]{0:T(128)S(1)}, s32[4]{0:T(128)}, u32[]{:S(2)}) copy-start(s32[4]{0:T(128)} %param.7) | copy-start | bytes 52
  20.0 98.8 %collective-permute-start.6 = (bf16[512,2048]{1,0:T(8,128)(2,1)}, bf16[512,2048]{1,0:T(8,128)(2,1)S(1)}, u32[]{:S(2)}, u32[]{:S(2)}) collective-permute-start(bf16[512,2048]{1,0:T(8,128)(2,1)} %slice.28), channel_id=1, source_target_pairs={{0,16},{16,0},{1,17},{17,1},{2,18},{18,2},{3,19},{19,3},{4,20},{20... | collective-permute-start | bytes 6291464 | tf_op jit(solution)/shard_map/ppermute | solution.py:214
  85.1 9.9 %copy-start.1 = (bf16[2,512,1024]{2,1,0:T(8,128)(2,1)S(1)}, bf16[2,512,1024]{2,1,0:T(8,128)(2,1)}, u32[]{:S(2)}) copy-start(bf16[2,512,1024]{2,1,0:T(8,128)(2,1)} %get-tuple-element.49) | copy-start | bytes 6291460
  85.1 10.9 %copy-start.2 = (bf16[512,512]{1,0:T(8,128)(2,1)S(1)}, bf16[512,512]{1,0:T(8,128)(2,1)}, u32[]{:S(2)}) copy-start(bf16[512,512]{1,0:T(8,128)(2,1)} %get-tuple-element.61) | copy-start | bytes 1572868
  95.1 46.1 %collective-permute-start.9 = (bf16[2,512,1024]{2,1,0:T(8,128)(2,1)S(1)}, bf16[2,512,1024]{2,1,0:T(8,128)(2,1)S(1)}, u32[]{:S(2)}, u32[]{:S(2)}) collective-permute-start(bf16[2,512,1024]{2,1,0:T(8,128)(2,1)S(1)} %copy-done.1), channel_id=1, source_target_pairs={{0,15},{1,2},{2,1},{3,4},{4,3},{5,6},{6,5},{7,8},{8,7},{9,10},{10,... | collective-permute-start | bytes 6291464 | tf_op jit(solution)/shard_map/ppermute | solution.py:200
  96.0 9.2 %collective-permute-start.3 = (bf16[512,512]{1,0:T(8,128)(2,1)S(1)}, bf16[512,512]{1,0:T(8,128)(2,1)S(1)}, u32[]{:S(2)}, u32[]{:S(2)}) collective-permute-start(bf16[512,512]{1,0:T(8,128)(2,1)S(1)} %copy-done.2), channel_id=1, source_target_pairs={{0,16},{16,0},{1,17},{17,1},{2,18},{18,2},{3,19},{19,3},{4,20},{20... | collective-permute-start | bytes 1572872 | tf_op jit(solution)/shard_map/ppermute | solution.py:214
  97.5 18.3 %collective-permute-start.5 = (bf16[512,640]{1,0:T(8,128)(2,1)S(1)}, bf16[512,640]{1,0:T(8,128)(2,1)S(1)}, u32[]{:S(2)}, u32[]{:S(2)}) collective-permute-start(bf16[512,640]{1,0:T(8,128)(2,1)S(1)} %get-tuple-element.39), channel_id=1, source_target_pairs={{0,16},{16,0},{1,17},{17,1},{2,18},{18,2},{3,19},{19,3},{4,20},{20... | collective-permute-start | bytes 1966088 | tf_op jit(solution)/shard_map/ppermute | solution.py:314
  114.2 20.8 %collective-permute-start.8 = (bf16[512,640]{1,0:T(8,128)(2,1)S(1)}, bf16[512,640]{1,0:T(8,128)(2,1)S(1)}, u32[]{:S(2)}, u32[]{:S(2)}) collective-permute-start(bf16[512,640]{1,0:T(8,128)(2,1)S(1)} %get-tuple-element.46), channel_id=1, source_target_pairs={{0,16},{16,0},{1,17},{17,1},{2,18},{18,2},{3,19},{19,3},{4,20},{20... | collective-permute-start | bytes 1966088 | tf_op jit(solution)/shard_map/ppermute | solution.py:314
  137.4 22.3 %collective-permute-start.11 = (bf16[512,1152]{1,0:T(8,128)(2,1)S(1)}, bf16[512,1152]{1,0:T(8,128)(2,1)S(1)}, u32[]{:S(2)}, u32[]{:S(2)}) collective-permute-start(bf16[512,1152]{1,0:T(8,128)(2,1)S(1)} %get-tuple-element.55), channel_id=1, source_target_pairs={{0,16},{16,0},{1,17},{17,1},{2,18},{18,2},{3,19},{19,3},{4,20},{20... | collective-permute-start | bytes 3538952 | tf_op jit(solution)/shard_map/ppermute | solution.py:314
  158.1 16.3 %collective-permute-start.10 = (bf16[512,1152]{1,0:T(8,128)(2,1)S(1)}, bf16[512,1152]{1,0:T(8,128)(2,1)S(1)}, u32[]{:S(2)}, u32[]{:S(2)}) collective-permute-start(bf16[512,1152]{1,0:T(8,128)(2,1)S(1)} %get-tuple-element.52), channel_id=1, source_target_pairs={{0,16},{16,0},{1,17},{17,1},{2,18},{18,2},{3,19},{19,3},{4,20},{20... | collective-permute-start | bytes 3538952 | tf_op jit(solution)/shard_map/ppermute | solution.py:314
